TPU v7x, 512 devices: a whole 4x8x8 slice. The times are simulated.
512 devices in a mesh: grp: 16 (over z, y_lo), ep: 32 (over x, y_hi, core).
Axes of the slice: x: 4, y: 8 (y_hi: 4, y_lo: 2; y = y_hi * 2 + y_lo), z: 8, core: 2. Of those that a mesh axis runs over, the one named last changes fastest.
Arguments:
- tokens: bfloat16 [65536, 2048], P(('grp', 'ep')), may hold values from -6 to 6
- norm_gain: float32 [2048], replicated, may hold values from 0.25 to 1.75
- w_gate: bfloat16 [32, 2048, 512], P('ep', 'grp'), may hold values from -0.125 to 0.125
- w_up: bfloat16 [32, 2048, 512], P('ep', 'grp'), may hold values from -0.125 to 0.125
- w_down: bfloat16 [32, 512, 2048], P('ep', None, 'grp'), may hold values from -0.25 to 0.25
- expert_ids: int32 [65536, 2], P(('grp', 'ep')), may hold values from 0 to 31, all different within a row; in each aligned block of 128 rows (0 to 127, 128 to 255, ...) at most 12 rows name the same one
- probs: float32 [65536, 2], P(('grp', 'ep')), may hold values from 0.1 to 1
- out_grad: bfloat16 [65536, 2048], P(('grp', 'ep')), may hold values from -6 to 6
Outputs:
- grad_tokens: bfloat16 [65536, 2048], P(('grp', 'ep'))
- grad_up: float32 [32, 2048, 512], P('ep', 'grp')
- grad_down: float32 [32, 512, 2048], P('ep', None, 'grp')
Inputs may be any that keep to these rules, and one draw needn't show every extreme that they name: `expert_ids`: each row names 2 different experts; among the 128 rows of one device, no expert is named by more than 12 rows, a bound that some block reaches.
All inputs are finite; a program needn't handle non-finite values.
Results may differ from a plain program's by a relative error of at most 0.017.
Values may be sent and summed in bfloat16 or wider, within the bound.
No kernel may reach another device: no remote copies, remote signals or barrier semaphores. Data moves between devices by JAX's collectives and lax.ppermute only.
A program may use at most 64 MiB of HBM per device.

v0:
```python
import functools
import math

import jax
import jax.numpy as jnp
from jax import lax
from jax.experimental import pallas as pl
from jax.experimental.pallas import tpu as pltpu
from jax.sharding import PartitionSpec as P


EPS = 1e-06
BF = jnp.bfloat16
F32 = jnp.float32


RING = 8
PAIR = 2
LOW = 8
HALF = 4


def shift_z(value, step):
    pairs = [
        (z * PAIR + y, ((z + step) % RING) * PAIR + y) for z in range(RING) for y in range(PAIR)
    ]
    return lax.ppermute(value, "grp", pairs)


def swap_y(value):
    pairs = [(z * PAIR + y, z * PAIR + 1 - y) for z in range(RING) for y in range(PAIR)]
    return lax.ppermute(value, "grp", pairs)


def near(*values):
    return [pltpu.with_memory_space_constraint(value, pltpu.VMEM) for value in values]


def far(*values):
    return [pltpu.with_memory_space_constraint(value, pltpu.HBM) for value in values]


def limit(mebibytes):
    return pltpu.CompilerParams(vmem_limit_bytes=mebibytes << 20)


def spot(index, step, other, rows):
    z, y = index >> 1, index & 1
    place = (((z + step) & (RING - 1)) << 1) | ((y + other) & (PAIR - 1))
    return pl.ds(pl.multiple_of(place * rows, rows), rows)


def dot(left, right, dims):
    return lax.dot_general(left, right, (dims, ((), ())), preferred_element_type=F32)


def dispatch_kernel(
    tokens, gain, ids, probs, out_grad, gate, up, down, send, select, shard
):
    rows, width = tokens.shape
    inner = gate.shape[1]
    shard[:, 0:inner] = gate[...]
    shard[:, inner : 2 * inner] = up[...]
    shard[:, 2 * inner : 3 * inner] = down[...].T
    experts = send.shape[0] // LOW
    token_f = tokens[...].astype(F32)
    inverse = lax.rsqrt(jnp.mean(token_f * token_f, axis=1, keepdims=True) + EPS)
    hidden = (token_f * inverse * gain[...]).astype(BF)
    expert = lax.broadcasted_iota(jnp.int32, (experts, rows), 0)
    first, second = ids[0:1, :] == expert, ids[1:2, :] == expert
    routed = jnp.where(first | second, 1.0, 0.0)
    weight = jnp.where(first, probs[0:1, :], 0.0) + jnp.where(second, probs[1:2, :], 0.0)
    earlier = lax.broadcasted_iota(jnp.int32, (rows, rows), 0) < lax.broadcasted_iota(
        jnp.int32, (rows, rows), 1
    )
    rank = dot(routed.astype(BF), jnp.where(earlier, 1.0, 0.0).astype(BF), ((1,), (0,)))
    slot = jnp.where(routed > 0.5, rank, -1.0)
    slot = jnp.broadcast_to(slot[:, None, :], (experts, LOW, rows))
    weight = jnp.broadcast_to(weight[:, None, :], (experts, LOW, rows))
    place = lax.broadcasted_iota(jnp.int32, (experts, LOW, rows), 1)
    low = jnp.where(slot == place.astype(F32), 1.0, 0.0)
    wanted = jnp.where(place < HALF, place + LOW, place + HALF).astype(F32)
    high = jnp.where(slot == wanted, 1.0, 0.0)
    flat = (experts * LOW, rows)
    low_scale = jnp.sum((low * weight).reshape(flat), axis=1, keepdims=True)
    high_scale = jnp.sum(
        jnp.where(place < HALF, high, high * weight).reshape(flat), axis=1, keepdims=True
    )
    low = low.reshape(flat).astype(BF)
    high_left = jnp.where(place < HALF, high, 0.0).reshape(flat).astype(BF)
    high_right = jnp.where(place < HALF, 0.0, high).reshape(flat).astype(BF)
    select[:, 0:rows] = low
    select[:, rows : 2 * rows] = high_left
    select[:, 2 * rows : 3 * rows] = high_right
    take = ((1,), (0,))
    send[:, 0:width] = dot(low, hidden, take).astype(BF)
    send[:, width : 2 * width] = (dot(low, out_grad[...], take) * low_scale).astype(BF)
    mixed = dot(high_left, hidden, take) + dot(high_right, out_grad[...], take)
    send[:, 2 * width : 3 * width] = (mixed * high_scale).astype(BF)


def turn(value):
    rows, width = value.shape
    value = value.reshape(rows // LOW, LOW, width)
    return pltpu.roll(value, HALF, 1).reshape(rows, width)


def expert_kernel(places, where, recv, *refs):
    count = len(places)
    blocks, refs = refs[:count], refs[count:]
    grad_pre, both, pieces, (last, parts, sems) = refs[0], refs[1], refs[2:-3], refs[-3:]
    rows = recv.shape[0]
    width = recv.shape[1] // 3
    inner = last.shape[1]
    index = where[0]
    block_rows = blocks[0].shape[0]
    copies = []
    for third in range(3):
        target = last if third == 2 else both.at[:, third * inner : (third + 1) * inner]
        copies.append([])
        for i, (step, other) in enumerate(places):
            copies[third].append(
                pltpu.make_async_copy(
                    blocks[i].at[:, third * inner : (third + 1) * inner],
                    target.at[spot(index, step, other, block_rows), :],
                    sems.at[third * count + i],
                )
            )
            copies[third][i].start()

    def arrived(third):
        for copy in copies[third]:
            copy.wait()

    upper = lax.broadcasted_iota(jnp.int32, (rows, inner), 0) % LOW < HALF
    low_h, low_c, mixed = (recv[:, i * width : (i + 1) * width] for i in range(3))
    row_col = ((1,), (0,))
    row_row = ((0,), (0,))

    def grads(pre_gate, pre_up, d_swiglu):
        sigmoid = jax.nn.sigmoid(pre_gate)
        act = pre_gate * sigmoid
        d_gate = d_swiglu * pre_up * sigmoid * (1.0 + pre_gate * (1.0 - sigmoid))
        return act * pre_up, d_gate, d_swiglu * act

    arrived(0)
    gate = both[:, 0:inner]
    pre_gate, pre_gate_x = dot(low_h, gate, row_col), dot(mixed, gate, row_col)
    arrived(1)
    up = both[:, inner : 2 * inner]
    pre_up, pre_up_x = dot(low_h, up, row_col), dot(mixed, up, row_col)
    arrived(2)
    down = last[...]
    d_swiglu, d_swiglu_x = dot(low_c, down, row_col), turn(dot(mixed, down, row_col))
    swiglu, d_gate, d_up = grads(pre_gate, pre_up, d_swiglu)
    swiglu_x, d_gate_x, d_up_x = grads(pre_gate_x, pre_up_x, d_swiglu_x)
    swiglu_x, d_gate_x, d_up_x = (jnp.where(upper, v, 0.0) for v in (swiglu_x, d_gate_x, d_up_x))
    d_up_b = d_up.astype(BF)
    parts[:, 0:inner] = (
        dot(low_h, d_up_b, row_row) + dot(mixed, d_up_x.astype(BF), row_row)
    ).astype(BF)
    parts[:, inner : 2 * inner] = (
        dot(low_c, swiglu.astype(BF), row_row) + dot(mixed, turn(swiglu_x).astype(BF), row_row)
    ).astype(BF)
    for i, value in enumerate((d_gate, d_up, d_gate_x + turn(d_gate_x), d_up_x + turn(d_up_x))):
        grad_pre[:, i * inner : (i + 1) * inner] = value.astype(BF)
    for (step, other), piece in zip(places, pieces, strict=True):
        piece[...] = parts[spot(index, step, other, block_rows), :]


def back_kernel(grad_pre, weights, back):
    rows = grad_pre.shape[0]
    width, both = weights.shape
    half = width // 2
    col_col = ((1,), (1,))
    back[:, 0:width] = dot(grad_pre[:, 0:both], weights[:, 0:both], col_col).astype(BF)
    high = grad_pre[:, both : 2 * both]
    left = dot(high, weights[0:half, 0:both], col_col)
    right = dot(high, weights[half:width, 0:both], col_col)
    pick = lax.broadcasted_iota(jnp.int32, (rows, half), 0) % LOW < HALF
    back[:, width : width + half] = jnp.where(pick, left, right).astype(BF)


def finish_kernel(tokens, gain, select, back, out):
    rows, width = tokens.shape
    half = width // 2
    token_f = tokens[...].astype(F32)
    inverse = lax.rsqrt(jnp.mean(token_f * token_f, axis=1, keepdims=True) + EPS)
    normed = token_f * inverse
    low, left, right = (select[:, i * rows : (i + 1) * rows] for i in range(3))
    row_row = ((0,), (0,))
    high = back[:, width : width + half]
    d_normed = dot(low, back[:, 0:width], row_row) + jnp.concatenate(
        [dot(left, high, row_row), dot(right, high, row_row)], axis=1
    )
    scaled = d_normed * gain[...]
    mean = jnp.mean(scaled * normed, axis=1, keepdims=True)
    out[...] = (inverse * (scaled - normed * mean)).astype(BF)


def last_kernel(factor, piece, first, second, away, grad_up, grad_down):
    inner = grad_up.shape[1]
    total = piece[...].astype(F32) + first[...].astype(F32) + second[...].astype(F32)
    total = (total + away[...].astype(F32)) * factor
    grad_up[...] = total[:, 0:inner]
    grad_down[...] = total[:, inner : 2 * inner].T


def gather_weights(shard):
    partner = swap_y(shard)
    found = {(0, 0): shard, (0, 1): partner}
    chains = [[shard, shard], [partner, partner]]
    middle = RING // 2
    for step in range(1, middle + 1):
        for other in range(PAIR):
            for way, sign in ((0, 1), (1, -1)):
                if step == middle and way != other:
                    continue
                chains[other][way] = shift_z(chains[other][way], sign)
                key = -sign * step if step < middle else middle
                found[key, other] = chains[other][way]
    return found


def scatter_parts(pieces, factor):
    rows, width = pieces[0, 0].shape
    inner = width // 2

    def add(*values):
        total = values[0].astype(F32)
        for value in values[1:]:
            total = total + value.astype(F32)
        return total.astype(BF)

    middle = RING // 2
    chains = {}
    for step in range(middle, 0, -1):
        for other in (1, 0):
            for way, sign in ((0, 1), (1, -1)):
                if step == middle and way != other:
                    continue
                block = pieces[sign * step if step < middle else middle, other]
                if (other, way) in chains:
                    block = add(block, chains[other, way])
                chains[other, way] = shift_z(block, sign)
    away = add(pieces[0, 1], chains[1, 0], chains[1, 1])
    away = swap_y(away)
    return pl.pallas_call(
        functools.partial(last_kernel, factor),
        out_shape=(
            jax.ShapeDtypeStruct((rows, inner), F32),
            jax.ShapeDtypeStruct((inner, rows), F32),
        ),
        compiler_params=limit(8),
        name="last",
    )(*near(pieces[0, 0], chains[0, 0], chains[0, 1], away))


def body(tokens, norm_gain, w_gate, w_up, w_down, expert_ids, probs, out_grad):
    rows, width = tokens.shape
    inner = w_gate.shape[2]
    experts = lax.axis_size("ep")
    gain = norm_gain.reshape(1, width)
    send, select, shard = pl.pallas_call(
        dispatch_kernel,
        out_shape=(
            jax.ShapeDtypeStruct((experts * LOW, 3 * width), BF),
            jax.ShapeDtypeStruct((experts * LOW, 3 * rows), BF),
            jax.ShapeDtypeStruct((rows, 3 * inner), BF),
        ),
        name="dispatch",
    )(tokens, gain, expert_ids.T, probs.T, out_grad, w_gate[0], w_up[0], w_down[0])
    found = gather_weights(shard)
    recv = lax.all_to_all(
        send.reshape(experts, LOW, 3 * width), "ep", split_axis=0, concat_axis=0, tiled=True
    ).reshape(experts * LOW, 3 * width)
    where = lax.axis_index("grp").astype(jnp.int32).reshape(1)
    places = tuple(found)
    grad_pre, both, *pieces = pl.pallas_call(
        functools.partial(expert_kernel, places),
        out_shape=[
            pltpu.VMEM((experts * LOW, 4 * inner), BF),
            pltpu.VMEM((width, 2 * inner), BF),
        ]
        + [pltpu.VMEM((rows, 2 * inner), BF)] * len(places),
        in_specs=[pl.BlockSpec(memory_space=pltpu.SMEM), pl.BlockSpec()]
        + [pl.BlockSpec(memory_space=pltpu.HBM)] * len(places),
        scratch_shapes=[
            pltpu.VMEM((width, inner), BF),
            pltpu.VMEM((width, 2 * inner), BF),
            pltpu.SemaphoreType.DMA((3 * len(places),)),
        ],
        compiler_params=limit(28),
        name="expert",
    )(where, *near(recv), *far(*found.values()))
    pieces = dict(zip(places, pieces, strict=True))
    back = pl.pallas_call(
        back_kernel,
        out_shape=jax.ShapeDtypeStruct((experts * LOW, width + width // 2), BF),
        compiler_params=limit(16),
        name="back",
    )(*near(grad_pre, both))
    back = lax.all_to_all(
        back.reshape(experts, LOW, width + width // 2),
        "ep",
        split_axis=0,
        concat_axis=0,
        tiled=True,
    ).reshape(experts * LOW, width + width // 2)
    factor = 1.0 / math.sqrt(
        rows * lax.axis_size("grp") * experts * expert_ids.shape[1] / experts
    )
    grad_up, grad_down = scatter_parts(pieces, factor)
    grad_tokens = pl.pallas_call(
        finish_kernel,
        out_shape=jax.ShapeDtypeStruct((rows, width), BF),
        compiler_params=limit(20),
        name="finish",
    )(tokens, gain, select, *near(back))
    return (grad_tokens, grad_up[None], grad_down[None])


def solution(mesh):
    in_specs = (
        P(("grp", "ep"), None),
        P(),
        P("ep", "grp", None),
        P("ep", "grp", None),
        P("ep", None, "grp"),
        P(("grp", "ep"), None),
        P(("grp", "ep"), None),
        P(("grp", "ep"), None),
    )
    out_specs = (P(("grp", "ep"), None), P("ep", "grp", None), P("ep", None, "grp"))
    return jax.shard_map(body, mesh=mesh, in_specs=in_specs, out_specs=out_specs, check_vma=False)
```

profile of v0, /device:TPU:6, one launch (start us, length us, event | category | flops | bytes accessed | tf_op | source)
XLA Modules:
  0.0 251.3 jit_solution(14397031053902985610)
XLA Ops:
  0.6 4.5 %dispatch.1 = (bf16[256,6144]{1,0:T(8,128)(2,1)}, bf16[256,384]{1,0:T(8,128)(2,1)}, bf16[128,1536]{1,0:T(8,128)(2,1)}) custom-call(bf16[128,2048]{1,0:T(8,128)(2,1)} %tokens.3, f32[1,2048]{1,0:T(1,128)} %bitcast.15, s32[2,128]{1,0:T(2,128)} %bitcast.21, f32[2,128]{1,0:T(2,128)} %bitcast.22, bf16[128,2048]{1,0:T(8,128)(2,1)} %out_grad.1, ...), custom_call_target="tpu_custom_call" | custom-call | tf_op jit(solution)/shard_map/dispatch/pallas_call | solution.py:264
  5.2 10.4 %all-to-all-start = ((bf16[32,8,6144]{2,1,0:T(8,128)(2,1)}), bf16[32,8,6144]{2,1,0:T(8,128)(2,1)S(1)}, u32[]{:S(2)}, u32[]{:S(2)}) async-start(bf16[32,8,6144]{2,1,0:T(8,128)(2,1)} %bitcast.17), calls=%async_computation | async-start | bytes 6291456 | tf_op jit(solution)/shard_map/all_to_all | solution.py:274
  15.6 2.6 %collective-permute-start = (bf16[128,1536]{1,0:T(8,128)(2,1)S(1)}, bf16[128,1536]{1,0:T(8,128)(2,1)S(1)}, u32[]{:S(2)}, u32[]{:S(2)}) collective-permute-start(bf16[128,1536]{1,0:T(8,128)(2,1)S(1)} %copy-done.22), channel_id=1, source_target_pairs={{0,32},{32,0},{64,96},{96,64},{128,160},{160,128},{192,224},{224,1... | collective-permute-start | bytes 1179656 | tf_op jit(solution)/shard_map/ppermute | solution.py:32
  18.2 4.3 %collective-permute-start.1 = (bf16[128,1536]{1,0:T(8,128)(2,1)S(1)}, bf16[128,1536]{1,0:T(8,128)(2,1)S(1)}, u32[]{:S(2)}, u32[]{:S(2)}) collective-permute-start(bf16[128,1536]{1,0:T(8,128)(2,1)S(1)} %copy-done.22), channel_id=1, source_target_pairs={{0,64},{32,96},{64,128},{96,160},{128,192},{160,224},{192,256},{22... | collective-permute-start | bytes 1179656 | tf_op jit(solution)/shard_map/ppermute | solution.py:27
  22.4 70.7 %collective-permute-done.refs_1_ = bf16[128,1536]{1,0:T(8,128)(2,1)S(1)} collective-permute-done((bf16[128,1536]{1,0:T(8,128)(2,1)S(1)}, bf16[128,1536]{1,0:T(8,128)(2,1)S(1)}, u32[]{:S(2)}, u32[]{:S(2)}) %collective-permute-start) | collective-permute-done | bytes 393248 | tf_op jit(solution)/shard_map/ppermute | solution.py:32
  93.2 10.9 %collective-permute-start.4 = (bf16[128,1536]{1,0:T(8,128)(2,1)S(1)}, bf16[128,1536]{1,0:T(8,128)(2,1)S(1)}, u32[]{:S(2)}, u32[]{:S(2)}) collective-permute-start(bf16[128,1536]{1,0:T(8,128)(2,1)S(1)} %collective-permute-done.refs_1_), channel_id=1, source_target_pairs={{0,448},{32,480},{64,0},{96,32},{128,64},{160,96},{192,128},{224,1... | collective-permute-start | bytes 1179656 | tf_op jit(solution)/shard_map/ppermute | solution.py:27
  104.1 2.5 collective-permute-start.2
  106.6 3.4 %collective-permute-start.5 = (bf16[128,1536]{1,0:T(8,128)(2,1)S(1)}, bf16[128,1536]{1,0:T(8,128)(2,1)S(1)}, u32[]{:S(2)}, u32[]{:S(2)}) collective-permute-start(bf16[128,1536]{1,0:T(8,128)(2,1)S(1)} %collective-permute-done.1.refs_2_), channel_id=1, source_target_pairs={{0,64},{32,96},{64,128},{96,160},{128,192},{160,224},{192,256},{22... | collective-permute-start | bytes 1179656 | tf_op jit(solution)/shard_map/ppermute | solution.py:27
  110.0 1.9 collective-permute-start.3
  111.9 1.7 collective-permute-done.4.refs_5_
  113.6 5.6 %collective-permute-start.8 = (bf16[128,1536]{1,0:T(8,128)(2,1)S(1)}, bf16[128,1536]{1,0:T(8,128)(2,1)S(1)}, u32[]{:S(2)}, u32[]{:S(2)}) collective-permute-start(bf16[128,1536]{1,0:T(8,128)(2,1)S(1)} %collective-permute-done.4.refs_5_), channel_id=1, source_target_pairs={{0,448},{32,480},{64,0},{96,32},{128,64},{160,96},{192,128},{224,1... | collective-permute-start | bytes 1179656 | tf_op jit(solution)/shard_map/ppermute | solution.py:27
  119.2 2.8 %collective-permute-done.2.refs_3_ = bf16[128,1536]{1,0:T(8,128)(2,1)S(1)} collective-permute-done((bf16[128,1536]{1,0:T(8,128)(2,1)S(1)}, bf16[128,1536]{1,0:T(8,128)(2,1)S(1)}, u32[]{:S(2)}, u32[]{:S(2)}) %collective-permute-start.2) | collective-permute-done | bytes 393248 | tf_op jit(solution)/shard_map/ppermute | solution.py:27
  122.0 5.6 %collective-permute-start.6 = (bf16[128,1536]{1,0:T(8,128)(2,1)S(1)}, bf16[128,1536]{1,0:T(8,128)(2,1)S(1)}, u32[]{:S(2)}, u32[]{:S(2)}) collective-permute-start(bf16[128,1536]{1,0:T(8,128)(2,1)S(1)} %collective-permute-done.2.refs_3_), channel_id=1, source_target_pairs={{0,448},{32,480},{64,0},{96,32},{128,64},{160,96},{192,128},{224,1... | collective-permute-start | bytes 1179656 | tf_op jit(solution)/shard_map/ppermute | solution.py:27
  127.7 1.9 collective-permute-start.9
  129.6 1.9 collective-permute-start.7
  131.6 5.1 %collective-permute-start.12 = (bf16[128,1536]{1,0:T(8,128)(2,1)S(1)}, bf16[128,1536]{1,0:T(8,128)(2,1)}, u32[]{:S(2)}, u32[]{:S(2)}) collective-permute-start(bf16[128,1536]{1,0:T(8,128)(2,1)S(1)} %collective-permute-done.8.refs_9_), channel_id=1, source_target_pairs={{0,448},{32,480},{64,0},{96,32},{128,64},{160,96},{192,128},{224,1... | collective-permute-start | bytes 1179656 | tf_op jit(solution)/shard_map/ppermute | solution.py:27
  136.7 2.2 collective-permute-done.6.refs_7_
  138.9 5.6 %collective-permute-start.10 = (bf16[128,1536]{1,0:T(8,128)(2,1)S(1)}, bf16[128,1536]{1,0:T(8,128)(2,1)}, u32[]{:S(2)}, u32[]{:S(2)}) collective-permute-start(bf16[128,1536]{1,0:T(8,128)(2,1)S(1)} %collective-permute-done.6.refs_7_), channel_id=1, source_target_pairs={{0,448},{32,480},{64,0},{96,32},{128,64},{160,96},{192,128},{224,1... | collective-permute-start | bytes 1179656 | tf_op jit(solution)/shard_map/ppermute | solution.py:27
  144.5 1.9 collective-permute-start.13
  146.4 0.9 collective-permute-done.7.refs_8_
  147.3 1.9 collective-permute-start.11
  149.2 5.1 %collective-permute-start.14 = (bf16[128,1536]{1,0:T(8,128)(2,1)}, bf16[128,1536]{1,0:T(8,128)(2,1)}, u32[]{:S(2)}, u32[]{:S(2)}) collective-permute-start(bf16[128,1536]{1,0:T(8,128)(2,1)} %collective-permute-done.12.refs_13_), channel_id=1, source_target_pairs={{0,448},{32,480},{64,0},{96,32},{128,64},{160,96},{192,128},{224,1... | collective-permute-start | bytes 1179656 | tf_op jit(solution)/shard_map/ppermute | solution.py:27
  154.4 1.4 collective-permute-done.10.refs_11_
  155.7 4.2 %collective-permute-done.13.refs_14_ = bf16[128,1536]{1,0:T(8,128)(2,1)} collective-permute-done((bf16[128,1536]{1,0:T(8,128)(2,1)}, bf16[128,1536]{1,0:T(8,128)(2,1)}, u32[]{:S(2)}, u32[]{:S(2)}) %collective-permute-start.13) | collective-permute-done | bytes 393248 | tf_op jit(solution)/shard_map/ppermute | solution.py:27
  159.9 4.4 %collective-permute-done.11.refs_12_ = bf16[128,1536]{1,0:T(8,128)(2,1)} collective-permute-done((bf16[128,1536]{1,0:T(8,128)(2,1)}, bf16[128,1536]{1,0:T(8,128)(2,1)}, u32[]{:S(2)}, u32[]{:S(2)}) %collective-permute-start.11) | collective-permute-done | bytes 393248 | tf_op jit(solution)/shard_map/ppermute | solution.py:27
  164.4 9.8 %expert.1 = (bf16[256,2048]{1,0:T(8,128)(2,1)S(1)}, bf16[2048,1024]{1,0:T(8,128)(2,1)S(1)}, bf16[128,1024]{1,0:T(8,128)(2,1)S(1)}, bf16[128,1024]{1,0:T(8,128)(2...) custom-call(s32[1]{0:T(128)} %bitcast.6.where, ...), custom_call_target="tpu_custom_call" | custom-call | tf_op jit(solution)/shard_map/expert/pallas_call | solution.py:279
  174.3 0.0 copy-start.16
  174.3 1.9 collective-permute-start.15
  176.2 3.6 %back.1 = bf16[256,3072]{1,0:T(8,128)(2,1)} custom-call(bf16[256,2048]{1,0:T(8,128)(2,1)S(1)} %get-tuple-element.29.grad_pre, bf16[2048,1024]{1,0:T(8,128)(2,1)S(1)} %get-tuple-element.30.weights), custom_call_target="tpu_custom_call" | custom-call | tf_op jit(solution)/shard_map/back/pallas_call | solution.py:297
  179.9 10.4 %all-to-all-start.1 = ((bf16[32,8,3072]{2,1,0:T(8,128)(2,1)}), bf16[32,8,3072]{2,1,0:T(8,128)(2,1)S(1)}, u32[]{:S(2)}, u32[]{:S(2)}) async-start(bf16[32,8,3072]{2,1,0:T(8,128)(2,1)} %bitcast.9), calls=%async_computation.1 | async-start | bytes 3145728 | tf_op jit(solution)/shard_map/all_to_all | solution.py:303
  190.3 5.3 %collective-permute-start.25 = (bf16[128,1024]{1,0:T(8,128)(2,1)}, bf16[128,1024]{1,0:T(8,128)(2,1)S(1)}, u32[]{:S(2)}, u32[]{:S(2)}) collective-permute-start(bf16[128,1024]{1,0:T(8,128)(2,1)} %get-tuple-element.46), channel_id=1, source_target_pairs={{0,448},{32,480},{64,0},{96,32},{128,64},{160,96},{192,128},{224,1... | collective-permute-start | bytes 786440 | tf_op jit(solution)/shard_map/ppermute | solution.py:27
  195.5 2.6 %collective-permute-start.19 = (bf16[128,1024]{1,0:T(8,128)(2,1)}, bf16[128,1024]{1,0:T(8,128)(2,1)S(1)}, u32[]{:S(2)}, u32[]{:S(2)}) collective-permute-start(bf16[128,1024]{1,0:T(8,128)(2,1)} %get-tuple-element.38), channel_id=1, source_target_pairs={{0,448},{32,480},{64,0},{96,32},{128,64},{160,96},{192,128},{224,1... | collective-permute-start | bytes 786440 | tf_op jit(solution)/shard_map/ppermute | solution.py:27
  198.2 3.2 %collective-permute-start.22 = (bf16[128,1024]{1,0:T(8,128)(2,1)}, bf16[128,1024]{1,0:T(8,128)(2,1)S(1)}, u32[]{:S(2)}, u32[]{:S(2)}) collective-permute-start(bf16[128,1024]{1,0:T(8,128)(2,1)} %get-tuple-element.42), channel_id=1, source_target_pairs={{0,64},{32,96},{64,128},{96,160},{128,192},{160,224},{192,256},{22... | collective-permute-start | bytes 786440 | tf_op jit(solution)/shard_map/ppermute | solution.py:27
  201.4 0.7 copy-done.31
  202.1 1.1 add_convert_fusion.10
  203.3 1.9 collective-permute-start.16
  205.2 1.0 add_convert_fusion.3
  206.2 5.1 %collective-permute-start.26 = (bf16[128,1024]{1,0:T(8,128)(2,1)S(1)}, bf16[128,1024]{1,0:T(8,128)(2,1)S(1)}, u32[]{:S(2)}, u32[]{:S(2)}) collective-permute-start(bf16[128,1024]{1,0:T(8,128)(2,1)S(1)} %add_convert_fusion.3), channel_id=1, source_target_pairs={{0,448},{32,480},{64,0},{96,32},{128,64},{160,96},{192,128},{224,1... | collective-permute-start | bytes 786440 | tf_op jit(solution)/shard_map/ppermute | solution.py:27
  211.4 1.1 add_convert_fusion.7
  212.5 2.6 %collective-permute-start.20 = (bf16[128,1024]{1,0:T(8,128)(2,1)S(1)}, bf16[128,1024]{1,0:T(8,128)(2,1)S(1)}, u32[]{:S(2)}, u32[]{:S(2)}) collective-permute-start(bf16[128,1024]{1,0:T(8,128)(2,1)S(1)} %add_convert_fusion.7), channel_id=1, source_target_pairs={{0,448},{32,480},{64,0},{96,32},{128,64},{160,96},{192,128},{224,1... | collective-permute-start | bytes 786440 | tf_op jit(solution)/shard_map/ppermute | solution.py:27
  215.1 0.0 copy-start.17
  215.1 0.1 add_convert_fusion.5
  215.2 3.2 %collective-permute-start.23 = (bf16[128,1024]{1,0:T(8,128)(2,1)S(1)}, bf16[128,1024]{1,0:T(8,128)(2,1)S(1)}, u32[]{:S(2)}, u32[]{:S(2)}) collective-permute-start(bf16[128,1024]{1,0:T(8,128)(2,1)S(1)} %add_convert_fusion.5), channel_id=1, source_target_pairs={{0,64},{32,96},{64,128},{96,160},{128,192},{160,224},{192,256},{22... | collective-permute-start | bytes 786440 | tf_op jit(solution)/shard_map/ppermute | solution.py:27
  218.4 0.1 add_convert_fusion.2
  218.5 0.0 copy-start
  218.5 0.0 copy-start.21
  218.5 5.3 %collective-permute-start.27 = (bf16[128,1024]{1,0:T(8,128)(2,1)S(1)}, bf16[128,1024]{1,0:T(8,128)(2,1)S(1)}, u32[]{:S(2)}, u32[]{:S(2)}) collective-permute-start(bf16[128,1024]{1,0:T(8,128)(2,1)S(1)} %add_convert_fusion.2), channel_id=1, source_target_pairs={{0,448},{32,480},{64,0},{96,32},{128,64},{160,96},{192,128},{224,1... | collective-permute-start | bytes 786440 | tf_op jit(solution)/shard_map/ppermute | solution.py:27
  223.9 0.1 add_convert_fusion.9
  224.0 1.9 collective-permute-start.17
  225.9 0.1 add_convert_fusion.4
  226.0 1.9 collective-permute-start.24
  228.0 0.1 add_convert_fusion.1
  228.0 5.4 %collective-permute-start.28 = (bf16[128,1024]{1,0:T(8,128)(2,1)S(1)}, bf16[128,1024]{1,0:T(8,128)(2,1)S(1)}, u32[]{:S(2)}, u32[]{:S(2)}) collective-permute-start(bf16[128,1024]{1,0:T(8,128)(2,1)S(1)} %add_convert_fusion.1), channel_id=1, source_target_pairs={{0,448},{32,480},{64,0},{96,32},{128,64},{160,96},{192,128},{224,1... | collective-permute-start | bytes 786440 | tf_op jit(solution)/shard_map/ppermute | solution.py:27
  233.5 0.1 add_convert_fusion.6
  233.5 3.7 %collective-permute-start.21 = (bf16[128,1024]{1,0:T(8,128)(2,1)S(1)}, bf16[128,1024]{1,0:T(8,128)(2,1)S(1)}, u32[]{:S(2)}, u32[]{:S(2)}) collective-permute-start(bf16[128,1024]{1,0:T(8,128)(2,1)S(1)} %add_convert_fusion.6), channel_id=1, source_target_pairs={{0,448},{32,480},{64,0},{96,32},{128,64},{160,96},{192,128},{224,1... | collective-permute-start | bytes 786440 | tf_op jit(solution)/shard_map/ppermute | solution.py:27
  237.2 0.1 add_convert_fusion.8
  237.3 2.2 collective-permute-start.18
  239.5 0.1 add_convert_fusion
  239.6 2.6 %collective-permute-start.29 = (bf16[128,1024]{1,0:T(8,128)(2,1)S(1)}, bf16[128,1024]{1,0:T(8,128)(2,1)S(1)}, u32[]{:S(2)}, u32[]{:S(2)}) collective-permute-start(bf16[128,1024]{1,0:T(8,128)(2,1)S(1)} %add_convert_fusion), channel_id=1, source_target_pairs={{0,32},{32,0},{64,96},{96,64},{128,160},{160,128},{192,224},{224,1... | collective-permute-start | bytes 786440 | tf_op jit(solution)/shard_map/ppermute | solution.py:32
  242.3 4.5 %collective-permute-done.18.first = bf16[128,1024]{1,0:T(8,128)(2,1)S(1)} collective-permute-done((bf16[128,1024]{1,0:T(8,128)(2,1)S(1)}, bf16[128,1024]{1,0:T(8,128)(2,1)S(1)}, u32[]{:S(2)}, u32[]{:S(2)}) %collective-permute-start.18) | collective-permute-done | bytes 262176 | tf_op jit(solution)/shard_map/ppermute | solution.py:27
  246.8 1.1 collective-permute-done.29.away
  247.9 1.0 last.1
  248.9 0.9 copy-done.20
  249.8 1.5 finish.1
  (80 shorter events, 0.2 us)
Async XLA Ops:
  5.2 10.4 %copy-start.22 = (bf16[128,1536]{1,0:T(8,128)(2,1)S(1)}, bf16[128,1536]{1,0:T(8,128)(2,1)}, u32[]{:S(2)}) copy-start(bf16[128,1536]{1,0:T(8,128)(2,1)} %get-tuple-element.28.refs_0_) | copy-start | bytes 1179652
  5.2 159.2 %all-to-all-start = ((bf16[32,8,6144]{2,1,0:T(8,128)(2,1)}), bf16[32,8,6144]{2,1,0:T(8,128)(2,1)S(1)}, u32[]{:S(2)}, u32[]{:S(2)}) async-start(bf16[32,8,6144]{2,1,0:T(8,128)(2,1)} %bitcast.17), calls=%async_computation | async-start | bytes 6291456 | tf_op jit(solution)/shard_map/all_to_all | solution.py:274
  15.6 77.6 %collective-permute-start = (bf16[128,1536]{1,0:T(8,128)(2,1)S(1)}, bf16[128,1536]{1,0:T(8,128)(2,1)S(1)}, u32[]{:S(2)}, u32[]{:S(2)}) collective-permute-start(bf16[128,1536]{1,0:T(8,128)(2,1)S(1)} %copy-done.22), channel_id=1, source_target_pairs={{0,32},{32,0},{64,96},{96,64},{128,160},{160,128},{192,224},{224,1... | collective-permute-start | bytes 1179656 | tf_op jit(solution)/shard_map/ppermute | solution.py:32
  18.2 88.4 %collective-permute-start.1 = (bf16[128,1536]{1,0:T(8,128)(2,1)S(1)}, bf16[128,1536]{1,0:T(8,128)(2,1)S(1)}, u32[]{:S(2)}, u32[]{:S(2)}) collective-permute-start(bf16[128,1536]{1,0:T(8,128)(2,1)S(1)} %copy-done.22), channel_id=1, source_target_pairs={{0,64},{32,96},{64,128},{96,160},{128,192},{160,224},{192,256},{22... | collective-permute-start | bytes 1179656 | tf_op jit(solution)/shard_map/ppermute | solution.py:27
  93.2 28.9 %copy-start.23 = (bf16[128,1536]{1,0:T(8,128)(2,1)}, bf16[128,1536]{1,0:T(8,128)(2,1)S(1)}, u32[]{:S(2)}) copy-start(bf16[128,1536]{1,0:T(8,128)(2,1)S(1)} %collective-permute-done.refs_1_) | copy-start | bytes 1179652
  93.2 20.4 %collective-permute-start.4 = (bf16[128,1536]{1,0:T(8,128)(2,1)S(1)}, bf16[128,1536]{1,0:T(8,128)(2,1)S(1)}, u32[]{:S(2)}, u32[]{:S(2)}) collective-permute-start(bf16[128,1536]{1,0:T(8,128)(2,1)S(1)} %collective-permute-done.refs_1_), channel_id=1, source_target_pairs={{0,448},{32,480},{64,0},{96,32},{128,64},{160,96},{192,128},{224,1... | collective-permute-start | bytes 1179656 | tf_op jit(solution)/shard_map/ppermute | solution.py:27
  104.1 17.9 %collective-permute-start.2 = (bf16[128,1536]{1,0:T(8,128)(2,1)S(1)}, bf16[128,1536]{1,0:T(8,128)(2,1)S(1)}, u32[]{:S(2)}, u32[]{:S(2)}) collective-permute-start(bf16[128,1536]{1,0:T(8,128)(2,1)S(1)} %copy-done.22), channel_id=1, source_target_pairs={{0,448},{32,480},{64,0},{96,32},{128,64},{160,96},{192,128},{224,1... | collective-permute-start | bytes 1179656 | tf_op jit(solution)/shard_map/ppermute | solution.py:27
  106.6 23.0 %copy-start.24 = (bf16[128,1536]{1,0:T(8,128)(2,1)}, bf16[128,1536]{1,0:T(8,128)(2,1)S(1)}, u32[]{:S(2)}) copy-start(bf16[128,1536]{1,0:T(8,128)(2,1)S(1)} %collective-permute-done.1.refs_2_) | copy-start | bytes 1179652
  106.6 21.0 %collective-permute-start.5 = (bf16[128,1536]{1,0:T(8,128)(2,1)S(1)}, bf16[128,1536]{1,0:T(8,128)(2,1)S(1)}, u32[]{:S(2)}, u32[]{:S(2)}) collective-permute-start(bf16[128,1536]{1,0:T(8,128)(2,1)S(1)} %collective-permute-done.1.refs_2_), channel_id=1, source_target_pairs={{0,64},{32,96},{64,128},{96,160},{128,192},{160,224},{192,256},{22... | collective-permute-start | bytes 1179656 | tf_op jit(solution)/shard_map/ppermute | solution.py:27
  110.0 19.6 %collective-permute-start.3 = (bf16[128,1536]{1,0:T(8,128)(2,1)S(1)}, bf16[128,1536]{1,0:T(8,128)(2,1)S(1)}, u32[]{:S(2)}, u32[]{:S(2)}) collective-permute-start(bf16[128,1536]{1,0:T(8,128)(2,1)S(1)} %collective-permute-done.refs_1_), channel_id=1, source_target_pairs={{0,64},{32,96},{64,128},{96,160},{128,192},{160,224},{192,256},{22... | collective-permute-start | bytes 1179656 | tf_op jit(solution)/shard_map/ppermute | solution.py:27
  113.6 17.9 %copy-start.25 = (bf16[128,1536]{1,0:T(8,128)(2,1)}, bf16[128,1536]{1,0:T(8,128)(2,1)S(1)}, u32[]{:S(2)}) copy-start(bf16[128,1536]{1,0:T(8,128)(2,1)S(1)} %collective-permute-done.4.refs_5_) | copy-start | bytes 1179652
  113.6 17.9 %collective-permute-start.8 = (bf16[128,1536]{1,0:T(8,128)(2,1)S(1)}, bf16[128,1536]{1,0:T(8,128)(2,1)S(1)}, u32[]{:S(2)}, u32[]{:S(2)}) collective-permute-start(bf16[128,1536]{1,0:T(8,128)(2,1)S(1)} %collective-permute-done.4.refs_5_), channel_id=1, source_target_pairs={{0,448},{32,480},{64,0},{96,32},{128,64},{160,96},{192,128},{224,1... | collective-permute-start | bytes 1179656 | tf_op jit(solution)/shard_map/ppermute | solution.py:27
  122.0 9.5 %copy-start.26 = (bf16[128,1536]{1,0:T(8,128)(2,1)}, bf16[128,1536]{1,0:T(8,128)(2,1)S(1)}, u32[]{:S(2)}) copy-start(bf16[128,1536]{1,0:T(8,128)(2,1)S(1)} %collective-permute-done.2.refs_3_) | copy-start | bytes 1179652
  122.0 16.8 %collective-permute-start.6 = (bf16[128,1536]{1,0:T(8,128)(2,1)S(1)}, bf16[128,1536]{1,0:T(8,128)(2,1)S(1)}, u32[]{:S(2)}, u32[]{:S(2)}) collective-permute-start(bf16[128,1536]{1,0:T(8,128)(2,1)S(1)} %collective-permute-done.2.refs_3_), channel_id=1, source_target_pairs={{0,448},{32,480},{64,0},{96,32},{128,64},{160,96},{192,128},{224,1... | collective-permute-start | bytes 1179656 | tf_op jit(solution)/shard_map/ppermute | solution.py:27
  127.6 11.2 %copy-start.27 = (bf16[128,1536]{1,0:T(8,128)(2,1)}, bf16[128,1536]{1,0:T(8,128)(2,1)S(1)}, u32[]{:S(2)}) copy-start(bf16[128,1536]{1,0:T(8,128)(2,1)S(1)} %collective-permute-done.5.refs_6_) | copy-start | bytes 1179652
  127.7 16.8 %collective-permute-start.9 = (bf16[128,1536]{1,0:T(8,128)(2,1)S(1)}, bf16[128,1536]{1,0:T(8,128)(2,1)}, u32[]{:S(2)}, u32[]{:S(2)}) collective-permute-start(bf16[128,1536]{1,0:T(8,128)(2,1)S(1)} %collective-permute-done.5.refs_6_), channel_id=1, source_target_pairs={{0,64},{32,96},{64,128},{96,160},{128,192},{160,224},{192,256},{22... | collective-permute-start | bytes 1179656 | tf_op jit(solution)/shard_map/ppermute | solution.py:27
  129.6 14.9 %copy-start.28 = (bf16[128,1536]{1,0:T(8,128)(2,1)}, bf16[128,1536]{1,0:T(8,128)(2,1)S(1)}, u32[]{:S(2)}) copy-start(bf16[128,1536]{1,0:T(8,128)(2,1)S(1)} %collective-permute-done.3.refs_4_) | copy-start | bytes 1179652
  129.6 17.7 %collective-permute-start.7 = (bf16[128,1536]{1,0:T(8,128)(2,1)S(1)}, bf16[128,1536]{1,0:T(8,128)(2,1)}, u32[]{:S(2)}, u32[]{:S(2)}) collective-permute-start(bf16[128,1536]{1,0:T(8,128)(2,1)S(1)} %collective-permute-done.3.refs_4_), channel_id=1, source_target_pairs={{0,64},{32,96},{64,128},{96,160},{128,192},{160,224},{192,256},{22... | collective-permute-start | bytes 1179656 | tf_op jit(solution)/shard_map/ppermute | solution.py:27
  131.6 15.7 %copy-start.29 = (bf16[128,1536]{1,0:T(8,128)(2,1)}, bf16[128,1536]{1,0:T(8,128)(2,1)S(1)}, u32[]{:S(2)}) copy-start(bf16[128,1536]{1,0:T(8,128)(2,1)S(1)} %collective-permute-done.8.refs_9_) | copy-start | bytes 1179652
  131.6 17.6 %collective-permute-start.12 = (bf16[128,1536]{1,0:T(8,128)(2,1)S(1)}, bf16[128,1536]{1,0:T(8,128)(2,1)}, u32[]{:S(2)}, u32[]{:S(2)}) collective-permute-start(bf16[128,1536]{1,0:T(8,128)(2,1)S(1)} %collective-permute-done.8.refs_9_), channel_id=1, source_target_pairs={{0,448},{32,480},{64,0},{96,32},{128,64},{160,96},{192,128},{224,1... | collective-permute-start | bytes 1179656 | tf_op jit(solution)/shard_map/ppermute | solution.py:27
  138.9 25.5 %copy-start.30 = (bf16[128,1536]{1,0:T(8,128)(2,1)}, bf16[128,1536]{1,0:T(8,128)(2,1)S(1)}, u32[]{:S(2)}) copy-start(bf16[128,1536]{1,0:T(8,128)(2,1)S(1)} %collective-permute-done.6.refs_7_) | copy-start | bytes 1179652
  138.9 16.8 %collective-permute-start.10 = (bf16[128,1536]{1,0:T(8,128)(2,1)S(1)}, bf16[128,1536]{1,0:T(8,128)(2,1)}, u32[]{:S(2)}, u32[]{:S(2)}) collective-permute-start(bf16[128,1536]{1,0:T(8,128)(2,1)S(1)} %collective-permute-done.6.refs_7_), channel_id=1, source_target_pairs={{0,448},{32,480},{64,0},{96,32},{128,64},{160,96},{192,128},{224,1... | collective-permute-start | bytes 1179656 | tf_op jit(solution)/shard_map/ppermute | solution.py:27
  144.5 15.4 %collective-permute-start.13 = (bf16[128,1536]{1,0:T(8,128)(2,1)}, bf16[128,1536]{1,0:T(8,128)(2,1)}, u32[]{:S(2)}, u32[]{:S(2)}) collective-permute-start(bf16[128,1536]{1,0:T(8,128)(2,1)} %collective-permute-done.9.refs_10_), channel_id=1, source_target_pairs={{0,64},{32,96},{64,128},{96,160},{128,192},{160,224},{192,256},{22... | collective-permute-start | bytes 1179656 | tf_op jit(solution)/shard_map/ppermute | solution.py:27
  147.3 17.1 %collective-permute-start.11 = (bf16[128,1536]{1,0:T(8,128)(2,1)}, bf16[128,1536]{1,0:T(8,128)(2,1)}, u32[]{:S(2)}, u32[]{:S(2)}) collective-permute-start(bf16[128,1536]{1,0:T(8,128)(2,1)} %collective-permute-done.7.refs_8_), channel_id=1, source_target_pairs={{0,64},{32,96},{64,128},{96,160},{128,192},{160,224},{192,256},{22... | collective-permute-start | bytes 1179656 | tf_op jit(solution)/shard_map/ppermute | solution.py:27
  149.2 15.1 %collective-permute-start.14 = (bf16[128,1536]{1,0:T(8,128)(2,1)}, bf16[128,1536]{1,0:T(8,128)(2,1)}, u32[]{:S(2)}, u32[]{:S(2)}) collective-permute-start(bf16[128,1536]{1,0:T(8,128)(2,1)} %collective-permute-done.12.refs_13_), channel_id=1, source_target_pairs={{0,448},{32,480},{64,0},{96,32},{128,64},{160,96},{192,128},{224,1... | collective-permute-start | bytes 1179656 | tf_op jit(solution)/shard_map/ppermute | solution.py:27
  174.2 5.6 %copy-start.1 = (bf16[128,1024]{1,0:T(8,128)(2,1)}, bf16[128,1024]{1,0:T(8,128)(2,1)S(1)}, u32[]{:S(2)}) copy-start(bf16[128,1024]{1,0:T(8,128)(2,1)S(1)} %get-tuple-element.36) | copy-start | bytes 786436
  174.2 5.6 %copy-start.3 = (bf16[128,1024]{1,0:T(8,128)(2,1)}, bf16[128,1024]{1,0:T(8,128)(2,1)S(1)}, u32[]{:S(2)}) copy-start(bf16[128,1024]{1,0:T(8,128)(2,1)S(1)} %get-tuple-element.43) | copy-start | bytes 786436
  174.2 5.6 %copy-start.5 = (bf16[128,1024]{1,0:T(8,128)(2,1)}, bf16[128,1024]{1,0:T(8,128)(2,1)S(1)}, u32[]{:S(2)}) copy-start(bf16[128,1024]{1,0:T(8,128)(2,1)S(1)} %get-tuple-element.40) | copy-start | bytes 786436
  174.2 5.6 %copy-start.7 = (bf16[128,1024]{1,0:T(8,128)(2,1)}, bf16[128,1024]{1,0:T(8,128)(2,1)S(1)}, u32[]{:S(2)}) copy-start(bf16[128,1024]{1,0:T(8,128)(2,1)S(1)} %get-tuple-element.33) | copy-start | bytes 786436
  174.2 5.6 %copy-start.9 = (bf16[128,1024]{1,0:T(8,128)(2,1)}, bf16[128,1024]{1,0:T(8,128)(2,1)S(1)}, u32[]{:S(2)}) copy-start(bf16[128,1024]{1,0:T(8,128)(2,1)S(1)} %get-tuple-element.44) | copy-start | bytes 786436
  174.2 5.6 %copy-start.11 = (bf16[128,1024]{1,0:T(8,128)(2,1)}, bf16[128,1024]{1,0:T(8,128)(2,1)S(1)}, u32[]{:S(2)}) copy-start(bf16[128,1024]{1,0:T(8,128)(2,1)S(1)} %get-tuple-element.41) | copy-start | bytes 786436
  174.2 5.6 %copy-start.13 = (bf16[128,1024]{1,0:T(8,128)(2,1)}, bf16[128,1024]{1,0:T(8,128)(2,1)S(1)}, u32[]{:S(2)}) copy-start(bf16[128,1024]{1,0:T(8,128)(2,1)S(1)} %get-tuple-element.37) | copy-start | bytes 786436
  174.2 5.6 %copy-start.14 = (bf16[128,1024]{1,0:T(8,128)(2,1)}, bf16[128,1024]{1,0:T(8,128)(2,1)S(1)}, u32[]{:S(2)}) copy-start(bf16[128,1024]{1,0:T(8,128)(2,1)S(1)} %get-tuple-element.45) | copy-start | bytes 786436
  174.2 5.6 %copy-start.15 = (bf16[128,1024]{1,0:T(8,128)(2,1)}, bf16[128,1024]{1,0:T(8,128)(2,1)S(1)}, u32[]{:S(2)}) copy-start(bf16[128,1024]{1,0:T(8,128)(2,1)S(1)} %get-tuple-element.34) | copy-start | bytes 786436
  174.3 5.6 %copy-start.16 = (bf16[128,1024]{1,0:T(8,128)(2,1)}, bf16[128,1024]{1,0:T(8,128)(2,1)S(1)}, u32[]{:S(2)}) copy-start(bf16[128,1024]{1,0:T(8,128)(2,1)S(1)} %get-tuple-element.31.piece) | copy-start | bytes 786436
  174.3 5.6 %copy-start.18 = (bf16[128,1024]{1,0:T(8,128)(2,1)}, bf16[128,1024]{1,0:T(8,128)(2,1)S(1)}, u32[]{:S(2)}) copy-start(bf16[128,1024]{1,0:T(8,128)(2,1)S(1)} %get-tuple-element.39) | copy-start | bytes 786436
  174.3 27.1 %collective-permute-start.15 = (bf16[128,1024]{1,0:T(8,128)(2,1)}, bf16[128,1024]{1,0:T(8,128)(2,1)S(1)}, u32[]{:S(2)}, u32[]{:S(2)}) collective-permute-start(bf16[128,1024]{1,0:T(8,128)(2,1)} %get-tuple-element.35), channel_id=1, source_target_pairs={{0,64},{32,96},{64,128},{96,160},{128,192},{160,224},{192,256},{22... | collective-permute-start | bytes 786440 | tf_op jit(solution)/shard_map/ppermute | solution.py:27
  179.8 35.3 %copy-start.12 = (bf16[128,1024]{1,0:T(8,128)(2,1)S(1)}, bf16[128,1024]{1,0:T(8,128)(2,1)}, u32[]{:S(2)}) copy-start(bf16[128,1024]{1,0:T(8,128)(2,1)} %copy-done.11) | copy-start | bytes 786436
  179.9 38.6 %copy-start.10 = (bf16[128,1024]{1,0:T(8,128)(2,1)S(1)}, bf16[128,1024]{1,0:T(8,128)(2,1)}, u32[]{:S(2)}) copy-start(bf16[128,1024]{1,0:T(8,128)(2,1)} %copy-done.9) | copy-start | bytes 786436
  179.9 44.0 %copy-start.8 = (bf16[128,1024]{1,0:T(8,128)(2,1)S(1)}, bf16[128,1024]{1,0:T(8,128)(2,1)}, u32[]{:S(2)}) copy-start(bf16[128,1024]{1,0:T(8,128)(2,1)} %copy-done.7) | copy-start | bytes 786436
  179.9 69.0 %all-to-all-start.1 = ((bf16[32,8,3072]{2,1,0:T(8,128)(2,1)}), bf16[32,8,3072]{2,1,0:T(8,128)(2,1)S(1)}, u32[]{:S(2)}, u32[]{:S(2)}) async-start(bf16[32,8,3072]{2,1,0:T(8,128)(2,1)} %bitcast.9), calls=%async_computation.1 | async-start | bytes 3145728 | tf_op jit(solution)/shard_map/all_to_all | solution.py:303
  190.2 35.7 %copy-start.6 = (bf16[128,1024]{1,0:T(8,128)(2,1)S(1)}, bf16[128,1024]{1,0:T(8,128)(2,1)}, u32[]{:S(2)}) copy-start(bf16[128,1024]{1,0:T(8,128)(2,1)} %copy-done.5) | copy-start | bytes 786436
  190.2 37.7 %copy-start.4 = (bf16[128,1024]{1,0:T(8,128)(2,1)S(1)}, bf16[128,1024]{1,0:T(8,128)(2,1)}, u32[]{:S(2)}) copy-start(bf16[128,1024]{1,0:T(8,128)(2,1)} %copy-done.3) | copy-start | bytes 786436
  190.3 14.9 %collective-permute-start.25 = (bf16[128,1024]{1,0:T(8,128)(2,1)}, bf16[128,1024]{1,0:T(8,128)(2,1)S(1)}, u32[]{:S(2)}, u32[]{:S(2)}) collective-permute-start(bf16[128,1024]{1,0:T(8,128)(2,1)} %get-tuple-element.46), channel_id=1, source_target_pairs={{0,448},{32,480},{64,0},{96,32},{128,64},{160,96},{192,128},{224,1... | collective-permute-start | bytes 786440 | tf_op jit(solution)/shard_map/ppermute | solution.py:27
  195.5 15.8 %collective-permute-start.19 = (bf16[128,1024]{1,0:T(8,128)(2,1)}, bf16[128,1024]{1,0:T(8,128)(2,1)S(1)}, u32[]{:S(2)}, u32[]{:S(2)}) collective-permute-start(bf16[128,1024]{1,0:T(8,128)(2,1)} %get-tuple-element.38), channel_id=1, source_target_pairs={{0,448},{32,480},{64,0},{96,32},{128,64},{160,96},{192,128},{224,1... | collective-permute-start | bytes 786440 | tf_op jit(solution)/shard_map/ppermute | solution.py:27
  198.2 16.9 %collective-permute-start.22 = (bf16[128,1024]{1,0:T(8,128)(2,1)}, bf16[128,1024]{1,0:T(8,128)(2,1)S(1)}, u32[]{:S(2)}, u32[]{:S(2)}) collective-permute-start(bf16[128,1024]{1,0:T(8,128)(2,1)} %get-tuple-element.42), channel_id=1, source_target_pairs={{0,64},{32,96},{64,128},{96,160},{128,192},{160,224},{192,256},{22... | collective-permute-start | bytes 786440 | tf_op jit(solution)/shard_map/ppermute | solution.py:27
  201.4 0.7 copy-start.31
  202.1 31.3 %copy-start.2 = (bf16[128,1024]{1,0:T(8,128)(2,1)S(1)}, bf16[128,1024]{1,0:T(8,128)(2,1)}, u32[]{:S(2)}) copy-start(bf16[128,1024]{1,0:T(8,128)(2,1)} %copy-done.1) | copy-start | bytes 786436
  203.3 20.6 %collective-permute-start.16 = (bf16[128,1024]{1,0:T(8,128)(2,1)S(1)}, bf16[128,1024]{1,0:T(8,128)(2,1)S(1)}, u32[]{:S(2)}, u32[]{:S(2)}) collective-permute-start(bf16[128,1024]{1,0:T(8,128)(2,1)S(1)} %add_convert_fusion.10), channel_id=1, source_target_pairs={{0,64},{32,96},{64,128},{96,160},{128,192},{160,224},{192,256},{22... | collective-permute-start | bytes 786440 | tf_op jit(solution)/shard_map/ppermute | solution.py:27
  206.2 12.2 %collective-permute-start.26 = (bf16[128,1024]{1,0:T(8,128)(2,1)S(1)}, bf16[128,1024]{1,0:T(8,128)(2,1)S(1)}, u32[]{:S(2)}, u32[]{:S(2)}) collective-permute-start(bf16[128,1024]{1,0:T(8,128)(2,1)S(1)} %add_convert_fusion.3), channel_id=1, source_target_pairs={{0,448},{32,480},{64,0},{96,32},{128,64},{160,96},{192,128},{224,1... | collective-permute-start | bytes 786440 | tf_op jit(solution)/shard_map/ppermute | solution.py:27
  211.4 28.1 %copy-start.19 = (bf16[128,1024]{1,0:T(8,128)(2,1)S(1)}, bf16[128,1024]{1,0:T(8,128)(2,1)}, u32[]{:S(2)}) copy-start(bf16[128,1024]{1,0:T(8,128)(2,1)} %copy-done.18) | copy-start | bytes 786436
  212.5 21.0 %collective-permute-start.20 = (bf16[128,1024]{1,0:T(8,128)(2,1)S(1)}, bf16[128,1024]{1,0:T(8,128)(2,1)S(1)}, u32[]{:S(2)}, u32[]{:S(2)}) collective-permute-start(bf16[128,1024]{1,0:T(8,128)(2,1)S(1)} %add_convert_fusion.7), channel_id=1, source_target_pairs={{0,448},{32,480},{64,0},{96,32},{128,64},{160,96},{192,128},{224,1... | collective-permute-start | bytes 786440 | tf_op jit(solution)/shard_map/ppermute | solution.py:27
  215.1 32.8 %copy-start.17 = (bf16[128,1024]{1,0:T(8,128)(2,1)S(1)}, bf16[128,1024]{1,0:T(8,128)(2,1)}, u32[]{:S(2)}) copy-start(bf16[128,1024]{1,0:T(8,128)(2,1)} %copy-done.16) | copy-start | bytes 786436
  215.2 10.7 %collective-permute-start.23 = (bf16[128,1024]{1,0:T(8,128)(2,1)S(1)}, bf16[128,1024]{1,0:T(8,128)(2,1)S(1)}, u32[]{:S(2)}, u32[]{:S(2)}) collective-permute-start(bf16[128,1024]{1,0:T(8,128)(2,1)S(1)} %add_convert_fusion.5), channel_id=1, source_target_pairs={{0,64},{32,96},{64,128},{96,160},{128,192},{160,224},{192,256},{22... | collective-permute-start | bytes 786440 | tf_op jit(solution)/shard_map/ppermute | solution.py:27
  218.5 30.4 %copy-start = (bf16[128,2048]{1,0:T(8,128)(2,1)S(1)}, bf16[128,2048]{1,0:T(8,128)(2,1)}, u32[]{:S(2)}) copy-start(bf16[128,2048]{1,0:T(8,128)(2,1)} %tokens.3) | copy-start | bytes 1572868
  218.5 30.4 %copy-start.21 = (f32[2048]{0:T(1024)S(1)}, f32[2048]{0:T(1024)}, u32[]{:S(2)}) copy-start(f32[2048]{0:T(1024)} %param.9) | copy-start | bytes 24580
  218.5 9.4 %collective-permute-start.27 = (bf16[128,1024]{1,0:T(8,128)(2,1)S(1)}, bf16[128,1024]{1,0:T(8,128)(2,1)S(1)}, u32[]{:S(2)}, u32[]{:S(2)}) collective-permute-start(bf16[128,1024]{1,0:T(8,128)(2,1)S(1)} %add_convert_fusion.2), channel_id=1, source_target_pairs={{0,448},{32,480},{64,0},{96,32},{128,64},{160,96},{192,128},{224,1... | collective-permute-start | bytes 786440 | tf_op jit(solution)/shard_map/ppermute | solution.py:27
  224.0 13.2 %collective-permute-start.17 = (bf16[128,1024]{1,0:T(8,128)(2,1)S(1)}, bf16[128,1024]{1,0:T(8,128)(2,1)S(1)}, u32[]{:S(2)}, u32[]{:S(2)}) collective-permute-start(bf16[128,1024]{1,0:T(8,128)(2,1)S(1)} %add_convert_fusion.9), channel_id=1, source_target_pairs={{0,64},{32,96},{64,128},{96,160},{128,192},{160,224},{192,256},{22... | collective-permute-start | bytes 786440 | tf_op jit(solution)/shard_map/ppermute | solution.py:27
  226.0 13.5 %collective-permute-start.24 = (bf16[128,1024]{1,0:T(8,128)(2,1)S(1)}, bf16[128,1024]{1,0:T(8,128)(2,1)S(1)}, u32[]{:S(2)}, u32[]{:S(2)}) collective-permute-start(bf16[128,1024]{1,0:T(8,128)(2,1)S(1)} %add_convert_fusion.4), channel_id=1, source_target_pairs={{0,64},{32,96},{64,128},{96,160},{128,192},{160,224},{192,256},{22... | collective-permute-start | bytes 786440 | tf_op jit(solution)/shard_map/ppermute | solution.py:27
  228.0 11.5 %collective-permute-start.28 = (bf16[128,1024]{1,0:T(8,128)(2,1)S(1)}, bf16[128,1024]{1,0:T(8,128)(2,1)S(1)}, u32[]{:S(2)}, u32[]{:S(2)}) collective-permute-start(bf16[128,1024]{1,0:T(8,128)(2,1)S(1)} %add_convert_fusion.1), channel_id=1, source_target_pairs={{0,448},{32,480},{64,0},{96,32},{128,64},{160,96},{192,128},{224,1... | collective-permute-start | bytes 786440 | tf_op jit(solution)/shard_map/ppermute | solution.py:27
  233.5 8.7 %collective-permute-start.21 = (bf16[128,1024]{1,0:T(8,128)(2,1)S(1)}, bf16[128,1024]{1,0:T(8,128)(2,1)S(1)}, u32[]{:S(2)}, u32[]{:S(2)}) collective-permute-start(bf16[128,1024]{1,0:T(8,128)(2,1)S(1)} %add_convert_fusion.6), channel_id=1, source_target_pairs={{0,448},{32,480},{64,0},{96,32},{128,64},{160,96},{192,128},{224,1... | collective-permute-start | bytes 786440 | tf_op jit(solution)/shard_map/ppermute | solution.py:27
  237.3 9.5 %collective-permute-start.18 = (bf16[128,1024]{1,0:T(8,128)(2,1)S(1)}, bf16[128,1024]{1,0:T(8,128)(2,1)S(1)}, u32[]{:S(2)}, u32[]{:S(2)}) collective-permute-start(bf16[128,1024]{1,0:T(8,128)(2,1)S(1)} %add_convert_fusion.8), channel_id=1, source_target_pairs={{0,64},{32,96},{64,128},{96,160},{128,192},{160,224},{192,256},{22... | collective-permute-start | bytes 786440 | tf_op jit(solution)/shard_map/ppermute | solution.py:27
  239.6 8.3 %collective-permute-start.29 = (bf16[128,1024]{1,0:T(8,128)(2,1)S(1)}, bf16[128,1024]{1,0:T(8,128)(2,1)S(1)}, u32[]{:S(2)}, u32[]{:S(2)}) collective-permute-start(bf16[128,1024]{1,0:T(8,128)(2,1)S(1)} %add_convert_fusion), channel_id=1, source_target_pairs={{0,32},{32,0},{64,96},{96,64},{128,160},{160,128},{192,224},{224,1... | collective-permute-start | bytes 786440 | tf_op jit(solution)/shard_map/ppermute | solution.py:32
  248.9 0.9 copy-start.20
where the time goes:
time: 253 us; the launch traced here: 251 us
  starting transfers between devices  130 us (51%)
  waiting for transfers between devices  93.9 us (37%)
  Pallas kernels  20.4 us (8%)
  other arithmetic  3.82 us (2%)
    ppermute x28, starting transfers between devices, shift_z(): return lax.ppermute(value, 'grp', pairs)  104 us
    ppermute x2, waiting for transfers between devices, swap_y(): return lax.ppermute(value, 'grp', pairs)  71.9 us
    ppermute x28, waiting for transfers between devices, shift_z(): return lax.ppermute(value, 'grp', pairs)  22.1 us
    all_to_all x1, starting transfers between devices, body(): lax.all_to_all(send.reshape(experts, LOW, 3 * width), 'ep', split_axis=0,...  10.4 us
    all_to_all x1, starting transfers between devices, body(): lax.all_to_all(back.reshape(experts, LOW, width + width // 2), 'ep', spli...  10.4 us
    pallas_call x1, Pallas kernels, body(): pl.pallas_call(functools.partial(expert_kernel, places), out_shape=[pltpu...  9.78 us
    ppermute x2, starting transfers between devices, swap_y(): return lax.ppermute(value, 'grp', pairs)  5.19 us
  transfers between devices with their start and end apart: 32, of which 10 were waited for; matrix products, arithmetic and copies ran while one was open for 2% of the time, Pallas kernels for 2%

commit v1 on v0

--- a/solution.py
+++ b/solution.py
@@ -54,15 +54,32 @@
     return lax.dot_general(left, right, (dims, ((), ())), preferred_element_type=F32)
 
 
-def dispatch_kernel(
-    tokens, gain, ids, probs, out_grad, gate, up, down, send, select, shard
-):
+def dispatch_kernel(*refs):
+    fars, (send_far, select_far, shard_far) = refs[:8], refs[8:11]
+    tokens, gain, ids, probs, out_grad, turned, send, select, shard, sems = refs[11:]
     rows, width = tokens.shape
-    inner = gate.shape[1]
-    shard[:, 0:inner] = gate[...]
-    shard[:, inner : 2 * inner] = up[...]
-    shard[:, 2 * inner : 3 * inner] = down[...].T
+    inner = turned.shape[0]
+    homes = (tokens, gain, ids, probs, out_grad)
+    homes += (shard.at[:, 0:inner], shard.at[:, inner : 2 * inner], turned)
+    loads = [
+        pltpu.make_async_copy(source, target, sems.at[i])
+        for i, (source, target) in enumerate(zip(fars, homes, strict=True))
+    ]
+    for i in (0, 2, 3, 1, 4, 7, 5, 6):
+        loads[i].start()
+    stores = []
+
+    def ship(source, target):
+        stores.append(pltpu.make_async_copy(source, target, sems.at[8 + len(stores)]))
+        stores[-1].start()
+
+    def ship_third(third):
+        here = slice(third * width, (third + 1) * width)
+        ship(send.at[:, here], send_far.at[:, here])
+
     experts = send.shape[0] // LOW
+    for i in (0, 1, 2, 3):
+        loads[i].wait()
     token_f = tokens[...].astype(F32)
     inverse = lax.rsqrt(jnp.mean(token_f * token_f, axis=1, keepdims=True) + EPS)
     hidden = (token_f * inverse * gain[...]).astype(BF)
@@ -94,9 +111,20 @@
     select[:, 2 * rows : 3 * rows] = high_right
     take = ((1,), (0,))
     send[:, 0:width] = dot(low, hidden, take).astype(BF)
+    ship_third(0)
+    loads[4].wait()
     send[:, width : 2 * width] = (dot(low, out_grad[...], take) * low_scale).astype(BF)
+    ship_third(1)
     mixed = dot(high_left, hidden, take) + dot(high_right, out_grad[...], take)
     send[:, 2 * width : 3 * width] = (mixed * high_scale).astype(BF)
+    ship_third(2)
+    for i in (5, 6, 7):
+        loads[i].wait()
+    shard[:, 2 * inner : 3 * inner] = turned[...].T
+    ship(shard, shard_far)
+    ship(select, select_far)
+    for copy in stores:
+        copy.wait()
 
 
 def turn(value):
@@ -198,12 +226,22 @@
     out[...] = (inverse * (scaled - normed * mean)).astype(BF)
 
 
-def last_kernel(factor, piece, first, second, away, grad_up, grad_down):
+def add_kernel(*refs):
+    total = refs[0][...].astype(F32)
+    for held in refs[1:-1]:
+        total = total + held[...].astype(F32)
+    refs[-1][...] = total.astype(BF)
+
+
+def mine_kernel(piece, first, second, total):
+    total[...] = piece[...].astype(F32) + first[...].astype(F32) + second[...].astype(F32)
+
+
+def last_kernel(factor, mine, away, grad_up, grad_down):
     inner = grad_up.shape[1]
-    total = piece[...].astype(F32) + first[...].astype(F32) + second[...].astype(F32)
-    total = (total + away[...].astype(F32)) * factor
-    grad_up[...] = total[:, 0:inner]
-    grad_down[...] = total[:, inner : 2 * inner].T
+    grad_up[...] = (mine[:, 0:inner] + away[:, 0:inner].astype(F32)) * factor
+    right = (mine[:, inner : 2 * inner] + away[:, inner : 2 * inner].astype(F32)) * factor
+    grad_down[...] = right.T
 
 
 def gather_weights(shard):
@@ -232,6 +270,14 @@
             total = total + value.astype(F32)
         return total.astype(BF)
 
+    def add_near(*values):
+        return pl.pallas_call(
+            add_kernel,
+            out_shape=pltpu.VMEM((rows, width), BF),
+            compiler_params=limit(2),
+            name="add",
+        )(*near(*values))
+
     middle = RING // 2
     chains = {}
     for step in range(middle, 0, -1):
@@ -241,19 +287,26 @@
                     continue
                 block = pieces[sign * step if step < middle else middle, other]
                 if (other, way) in chains:
-                    block = add(block, chains[other, way])
+                    late = step == 1 or (step == 2 and way == other)
+                    block = (add_near if late else add)(block, chains[other, way])
                 chains[other, way] = shift_z(block, sign)
-    away = add(pieces[0, 1], chains[1, 0], chains[1, 1])
+    away = add_near(pieces[0, 1], chains[1, 0], chains[1, 1])
     away = swap_y(away)
+    mine = pl.pallas_call(
+        mine_kernel,
+        out_shape=pltpu.VMEM((rows, width), F32),
+        compiler_params=limit(2),
+        name="mine",
+    )(*near(pieces[0, 0], chains[0, 0], chains[0, 1]))
     return pl.pallas_call(
         functools.partial(last_kernel, factor),
         out_shape=(
             jax.ShapeDtypeStruct((rows, inner), F32),
             jax.ShapeDtypeStruct((inner, rows), F32),
         ),
-        compiler_params=limit(8),
+        compiler_params=limit(4),
         name="last",
-    )(*near(pieces[0, 0], chains[0, 0], chains[0, 1], away))
+    )(*near(mine, away))
 
 
 def body(tokens, norm_gain, w_gate, w_up, w_down, expert_ids, probs, out_grad):
@@ -261,6 +314,7 @@
     inner = w_gate.shape[2]
     experts = lax.axis_size("ep")
     gain = norm_gain.reshape(1, width)
+    there = pl.BlockSpec(memory_space=pltpu.HBM)
     send, select, shard = pl.pallas_call(
         dispatch_kernel,
         out_shape=(
@@ -268,8 +322,22 @@
             jax.ShapeDtypeStruct((experts * LOW, 3 * rows), BF),
             jax.ShapeDtypeStruct((rows, 3 * inner), BF),
         ),
+        in_specs=[there] * 8,
+        out_specs=(there, there, there),
+        scratch_shapes=[
+            pltpu.VMEM((rows, width), BF),
+            pltpu.VMEM((1, width), F32),
+            pltpu.VMEM((2, rows), jnp.int32),
+            pltpu.VMEM((2, rows), F32),
+            pltpu.VMEM((rows, width), BF),
+            pltpu.VMEM((inner, rows), BF),
+            pltpu.VMEM((experts * LOW, 3 * width), BF),
+            pltpu.VMEM((experts * LOW, 3 * rows), BF),
+            pltpu.VMEM((rows, 3 * inner), BF),
+            pltpu.SemaphoreType.DMA((13,)),
+        ],
         name="dispatch",
-    )(tokens, gain, expert_ids.T, probs.T, out_grad, w_gate[0], w_up[0], w_down[0])
+    )(*far(tokens, gain, expert_ids.T, probs.T, out_grad, w_gate[0], w_up[0], w_down[0]))
     found = gather_weights(shard)
     recv = lax.all_to_all(
         send.reshape(experts, LOW, 3 * width), "ep", split_axis=0, concat_axis=0, tiled=True

time: 253 us -> 248 us (0.980)
  other arithmetic: 3.82 us -> 0.27 us
    convert_element_type x11 -> x4, other arithmetic: 3.82 us -> 0.27 us  [add(): return total.astype(BF)]
  transfers between devices with their start and end apart: 32 -> 32, of which waited for: 10 -> 11; matrix products, arithmetic and copies ran while one was open for 2% -> 0% of each run, Pallas kernels for 2% -> 1%
where the time goes in v1:
time: 248 us; the launch traced here: 247 us
  starting transfers between devices  129 us (52%)
  waiting for transfers between devices  95.6 us (39%)
  Pallas kernels  19.4 us (8%)
    ppermute x28, starting transfers between devices, shift_z(): return lax.ppermute(value, 'grp', pairs)  104 us
    ppermute x2, waiting for transfers between devices, swap_y(): return lax.ppermute(value, 'grp', pairs)  73.1 us
    ppermute x28, waiting for transfers between devices, shift_z(): return lax.ppermute(value, 'grp', pairs)  22.5 us
    all_to_all x1, starting transfers between devices, body(): lax.all_to_all(send.reshape(experts, LOW, 3 * width), 'ep', split_axis=0,...  10.2 us
    all_to_all x1, starting transfers between devices, body(): lax.all_to_all(back.reshape(experts, LOW, width + width // 2), 'ep', spli...  10.2 us
    pallas_call x1, Pallas kernels, body(): pl.pallas_call(functools.partial(expert_kernel, places), out_shape=[pltpu...  8.95 us
    ppermute x2, starting transfers between devices, swap_y(): return lax.ppermute(value, 'grp', pairs)  5.13 us
  transfers between devices with their start and end apart: 32, of which 11 were waited for; matrix products, arithmetic and copies ran while one was open for 0% of the time, Pallas kernels for 1%

profile of v1, /device:TPU:6, one launch (start us, length us, event | category | flops | bytes accessed | tf_op | source)
XLA Modules:
  0.0 247.2 jit_solution(5277613125654951070)
XLA Ops:
  0.6 3.9 %dispatch.1 = (bf16[256,6144]{1,0:T(8,128)(2,1)}, bf16[256,384]{1,0:T(8,128)(2,1)}, bf16[128,1536]{1,0:T(8,128)(2,1)}) custom-call(bf16[128,2048]{1,0:T(8,128)(2,1)} %tokens.1, f32[1,2048]{1,0:T(1,128)} %bitcast.15, s32[2,128]{1,0:T(2,128)} %bitcast.21, f32[2,128]{1,0:T(2,128)} %bitcast.22, bf16[128,2048]{1,0:T(8,128)(2,1)} %refs_4_.1, ...), custom_call_target="tpu_custom_call" | custom-call | tf_op jit(solution)/shard_map/dispatch/pallas_call | solution.py:318
  4.6 10.2 %all-to-all-start = ((bf16[32,8,6144]{2,1,0:T(8,128)(2,1)}), bf16[32,8,6144]{2,1,0:T(8,128)(2,1)S(1)}, u32[]{:S(2)}, u32[]{:S(2)}) async-start(bf16[32,8,6144]{2,1,0:T(8,128)(2,1)} %bitcast.17), calls=%async_computation | async-start | bytes 6291456 | tf_op jit(solution)/shard_map/all_to_all | solution.py:342
  14.8 2.6 %collective-permute-start = (bf16[128,1536]{1,0:T(8,128)(2,1)}, bf16[128,1536]{1,0:T(8,128)(2,1)S(1)}, u32[]{:S(2)}, u32[]{:S(2)}) collective-permute-start(bf16[128,1536]{1,0:T(8,128)(2,1)} %get-tuple-element.28.refs_0_), channel_id=1, source_target_pairs={{0,32},{32,0},{64,96},{96,64},{128,160},{160,128},{192,224},{224,1... | collective-permute-start | bytes 1179656 | tf_op jit(solution)/shard_map/ppermute | solution.py:32
  17.4 4.3 %collective-permute-start.1 = (bf16[128,1536]{1,0:T(8,128)(2,1)}, bf16[128,1536]{1,0:T(8,128)(2,1)S(1)}, u32[]{:S(2)}, u32[]{:S(2)}) collective-permute-start(bf16[128,1536]{1,0:T(8,128)(2,1)} %get-tuple-element.28.refs_0_), channel_id=1, source_target_pairs={{0,64},{32,96},{64,128},{96,160},{128,192},{160,224},{192,256},{22... | collective-permute-start | bytes 1179656 | tf_op jit(solution)/shard_map/ppermute | solution.py:27
  21.7 70.8 %collective-permute-done.refs_1_ = bf16[128,1536]{1,0:T(8,128)(2,1)S(1)} collective-permute-done((bf16[128,1536]{1,0:T(8,128)(2,1)}, bf16[128,1536]{1,0:T(8,128)(2,1)S(1)}, u32[]{:S(2)}, u32[]{:S(2)}) %collective-permute-start) | collective-permute-done | bytes 393248 | tf_op jit(solution)/shard_map/ppermute | solution.py:32
  92.5 10.9 %collective-permute-start.4 = (bf16[128,1536]{1,0:T(8,128)(2,1)S(1)}, bf16[128,1536]{1,0:T(8,128)(2,1)S(1)}, u32[]{:S(2)}, u32[]{:S(2)}) collective-permute-start(bf16[128,1536]{1,0:T(8,128)(2,1)S(1)} %collective-permute-done.refs_1_), channel_id=1, source_target_pairs={{0,448},{32,480},{64,0},{96,32},{128,64},{160,96},{192,128},{224,1... | collective-permute-start | bytes 1179656 | tf_op jit(solution)/shard_map/ppermute | solution.py:27
  103.4 2.5 collective-permute-start.2
  105.9 3.4 %collective-permute-start.5 = (bf16[128,1536]{1,0:T(8,128)(2,1)S(1)}, bf16[128,1536]{1,0:T(8,128)(2,1)S(1)}, u32[]{:S(2)}, u32[]{:S(2)}) collective-permute-start(bf16[128,1536]{1,0:T(8,128)(2,1)S(1)} %collective-permute-done.1.refs_2_), channel_id=1, source_target_pairs={{0,64},{32,96},{64,128},{96,160},{128,192},{160,224},{192,256},{22... | collective-permute-start | bytes 1179656 | tf_op jit(solution)/shard_map/ppermute | solution.py:27
  109.3 1.9 collective-permute-start.3
  111.2 1.7 collective-permute-done.4.refs_5_
  112.9 5.6 %collective-permute-start.8 = (bf16[128,1536]{1,0:T(8,128)(2,1)S(1)}, bf16[128,1536]{1,0:T(8,128)(2,1)S(1)}, u32[]{:S(2)}, u32[]{:S(2)}) collective-permute-start(bf16[128,1536]{1,0:T(8,128)(2,1)S(1)} %collective-permute-done.4.refs_5_), channel_id=1, source_target_pairs={{0,448},{32,480},{64,0},{96,32},{128,64},{160,96},{192,128},{224,1... | collective-permute-start | bytes 1179656 | tf_op jit(solution)/shard_map/ppermute | solution.py:27
  118.5 2.9 %collective-permute-done.2.refs_3_ = bf16[128,1536]{1,0:T(8,128)(2,1)S(1)} collective-permute-done((bf16[128,1536]{1,0:T(8,128)(2,1)}, bf16[128,1536]{1,0:T(8,128)(2,1)S(1)}, u32[]{:S(2)}, u32[]{:S(2)}) %collective-permute-start.2) | collective-permute-done | bytes 393248 | tf_op jit(solution)/shard_map/ppermute | solution.py:27
  121.4 5.5 %collective-permute-start.6 = (bf16[128,1536]{1,0:T(8,128)(2,1)S(1)}, bf16[128,1536]{1,0:T(8,128)(2,1)}, u32[]{:S(2)}, u32[]{:S(2)}) collective-permute-start(bf16[128,1536]{1,0:T(8,128)(2,1)S(1)} %collective-permute-done.2.refs_3_), channel_id=1, source_target_pairs={{0,448},{32,480},{64,0},{96,32},{128,64},{160,96},{192,128},{224,1... | collective-permute-start | bytes 1179656 | tf_op jit(solution)/shard_map/ppermute | solution.py:27
  126.9 1.9 collective-permute-start.9
  128.9 1.9 collective-permute-start.7
  130.9 5.1 %collective-permute-start.12 = (bf16[128,1536]{1,0:T(8,128)(2,1)S(1)}, bf16[128,1536]{1,0:T(8,128)(2,1)}, u32[]{:S(2)}, u32[]{:S(2)}) collective-permute-start(bf16[128,1536]{1,0:T(8,128)(2,1)S(1)} %collective-permute-done.8.refs_9_), channel_id=1, source_target_pairs={{0,448},{32,480},{64,0},{96,32},{128,64},{160,96},{192,128},{224,1... | collective-permute-start | bytes 1179656 | tf_op jit(solution)/shard_map/ppermute | solution.py:27
  136.0 2.2 collective-permute-done.6.refs_7_
  138.2 5.7 %collective-permute-start.10 = (bf16[128,1536]{1,0:T(8,128)(2,1)}, bf16[128,1536]{1,0:T(8,128)(2,1)}, u32[]{:S(2)}, u32[]{:S(2)}) collective-permute-start(bf16[128,1536]{1,0:T(8,128)(2,1)} %collective-permute-done.6.refs_7_), channel_id=1, source_target_pairs={{0,448},{32,480},{64,0},{96,32},{128,64},{160,96},{192,128},{224,1... | collective-permute-start | bytes 1179656 | tf_op jit(solution)/shard_map/ppermute | solution.py:27
  143.9 1.9 collective-permute-start.13
  145.8 0.8 collective-permute-done.7.refs_8_
  146.6 1.9 collective-permute-start.11
  148.5 5.1 %collective-permute-start.14 = (bf16[128,1536]{1,0:T(8,128)(2,1)}, bf16[128,1536]{1,0:T(8,128)(2,1)}, u32[]{:S(2)}, u32[]{:S(2)}) collective-permute-start(bf16[128,1536]{1,0:T(8,128)(2,1)} %collective-permute-done.12.refs_13_), channel_id=1, source_target_pairs={{0,448},{32,480},{64,0},{96,32},{128,64},{160,96},{192,128},{224,1... | collective-permute-start | bytes 1179656 | tf_op jit(solution)/shard_map/ppermute | solution.py:27
  153.7 1.5 collective-permute-done.10.refs_11_
  155.1 4.2 %collective-permute-done.13.refs_14_ = bf16[128,1536]{1,0:T(8,128)(2,1)} collective-permute-done((bf16[128,1536]{1,0:T(8,128)(2,1)}, bf16[128,1536]{1,0:T(8,128)(2,1)}, u32[]{:S(2)}, u32[]{:S(2)}) %collective-permute-start.13) | collective-permute-done | bytes 393248 | tf_op jit(solution)/shard_map/ppermute | solution.py:27
  159.3 4.4 %collective-permute-done.11.refs_12_ = bf16[128,1536]{1,0:T(8,128)(2,1)} collective-permute-done((bf16[128,1536]{1,0:T(8,128)(2,1)}, bf16[128,1536]{1,0:T(8,128)(2,1)}, u32[]{:S(2)}, u32[]{:S(2)}) %collective-permute-start.11) | collective-permute-done | bytes 393248 | tf_op jit(solution)/shard_map/ppermute | solution.py:27
  163.8 9.0 %expert.1 = (bf16[256,2048]{1,0:T(8,128)(2,1)S(1)}, bf16[2048,1024]{1,0:T(8,128)(2,1)S(1)}, bf16[128,1024]{1,0:T(8,128)(2,1)S(1)}, bf16[128,1024]{1,0:T(8,128)(2...) custom-call(s32[1]{0:T(128)} %bitcast.6.where, ...), custom_call_target="tpu_custom_call" | custom-call | tf_op jit(solution)/shard_map/expert/pallas_call | solution.py:347
  172.7 0.0 copy-start.1
  172.9 3.6 %back.1 = bf16[256,3072]{1,0:T(8,128)(2,1)} custom-call(bf16[256,2048]{1,0:T(8,128)(2,1)S(1)} %get-tuple-element.29.grad_pre, bf16[2048,1024]{1,0:T(8,128)(2,1)S(1)} %get-tuple-element.30.weights), custom_call_target="tpu_custom_call" | custom-call | tf_op jit(solution)/shard_map/back/pallas_call | solution.py:365
  176.6 0.0 copy-start.10
  176.6 10.2 %all-to-all-start.1 = ((bf16[32,8,3072]{2,1,0:T(8,128)(2,1)}), bf16[32,8,3072]{2,1,0:T(8,128)(2,1)S(1)}, u32[]{:S(2)}, u32[]{:S(2)}) async-start(bf16[32,8,3072]{2,1,0:T(8,128)(2,1)} %bitcast.9), calls=%async_computation.1 | async-start | bytes 3145728 | tf_op jit(solution)/shard_map/all_to_all | solution.py:371
  186.8 3.9 %collective-permute-start.25 = (bf16[128,1024]{1,0:T(8,128)(2,1)}, bf16[128,1024]{1,0:T(8,128)(2,1)S(1)}, u32[]{:S(2)}, u32[]{:S(2)}) collective-permute-start(bf16[128,1024]{1,0:T(8,128)(2,1)} %copy-done.29), channel_id=1, source_target_pairs={{0,448},{32,480},{64,0},{96,32},{128,64},{160,96},{192,128},{224,1... | collective-permute-start | bytes 786440 | tf_op jit(solution)/shard_map/ppermute | solution.py:27
  190.7 2.1 collective-permute-start.15
  192.8 5.0 %collective-permute-start.19 = (bf16[128,1024]{1,0:T(8,128)(2,1)S(1)}, bf16[128,1024]{1,0:T(8,128)(2,1)S(1)}, u32[]{:S(2)}, u32[]{:S(2)}) collective-permute-start(bf16[128,1024]{1,0:T(8,128)(2,1)S(1)} %copy-done.26), channel_id=1, source_target_pairs={{0,448},{32,480},{64,0},{96,32},{128,64},{160,96},{192,128},{224,1... | collective-permute-start | bytes 786440 | tf_op jit(solution)/shard_map/ppermute | solution.py:27
  197.8 1.9 collective-permute-start.22
  199.8 0.1 add_convert_fusion
  199.9 5.1 %collective-permute-start.26 = (bf16[128,1024]{1,0:T(8,128)(2,1)S(1)}, bf16[128,1024]{1,0:T(8,128)(2,1)S(1)}, u32[]{:S(2)}, u32[]{:S(2)}) collective-permute-start(bf16[128,1024]{1,0:T(8,128)(2,1)S(1)} %add_convert_fusion), channel_id=1, source_target_pairs={{0,448},{32,480},{64,0},{96,32},{128,64},{160,96},{192,128},{224,1... | collective-permute-start | bytes 786440 | tf_op jit(solution)/shard_map/ppermute | solution.py:27
  205.0 0.1 add_convert_fusion.3
  205.1 1.9 collective-permute-start.16
  207.0 1.6 collective-permute-done.22
  208.6 0.1 add_convert_fusion.1
  208.7 1.9 collective-permute-start.23
  210.7 0.9 copy-done.14
  211.6 0.1 add.31
  211.7 5.1 %collective-permute-start.27 = (bf16[128,1024]{1,0:T(8,128)(2,1)S(1)}, bf16[128,1024]{1,0:T(8,128)(2,1)S(1)}, u32[]{:S(2)}, u32[]{:S(2)}) collective-permute-start(bf16[128,1024]{1,0:T(8,128)(2,1)S(1)} %add.31), channel_id=1, source_target_pairs={{0,448},{32,480},{64,0},{96,32},{128,64},{160,96},{192,128},{224,1... | collective-permute-start | bytes 786440 | tf_op jit(solution)/shard_map/ppermute | solution.py:27
  216.8 0.1 add_convert_fusion.2
  216.9 2.4 collective-permute-start.20
  219.3 0.1 add.27
  219.4 3.5 %collective-permute-start.17 = (bf16[128,1024]{1,0:T(8,128)(2,1)S(1)}, bf16[128,1024]{1,0:T(8,128)(2,1)S(1)}, u32[]{:S(2)}, u32[]{:S(2)}) collective-permute-start(bf16[128,1024]{1,0:T(8,128)(2,1)S(1)} %add.27), channel_id=1, source_target_pairs={{0,64},{32,96},{64,128},{96,160},{128,192},{160,224},{192,256},{22... | collective-permute-start | bytes 786440 | tf_op jit(solution)/shard_map/ppermute | solution.py:27
  222.9 0.1 add.30
  223.0 2.1 collective-permute-start.24
  225.1 0.1 add.32
  225.1 5.1 %collective-permute-start.28 = (bf16[128,1024]{1,0:T(8,128)(2,1)S(1)}, bf16[128,1024]{1,0:T(8,128)(2,1)S(1)}, u32[]{:S(2)}, u32[]{:S(2)}) collective-permute-start(bf16[128,1024]{1,0:T(8,128)(2,1)S(1)} %add.32), channel_id=1, source_target_pairs={{0,448},{32,480},{64,0},{96,32},{128,64},{160,96},{192,128},{224,1... | collective-permute-start | bytes 786440 | tf_op jit(solution)/shard_map/ppermute | solution.py:27
  230.3 0.1 add.29
  230.4 2.4 collective-permute-start.21
  232.8 0.1 add.28
  232.8 3.5 %collective-permute-start.18 = (bf16[128,1024]{1,0:T(8,128)(2,1)S(1)}, bf16[128,1024]{1,0:T(8,128)(2,1)S(1)}, u32[]{:S(2)}, u32[]{:S(2)}) collective-permute-start(bf16[128,1024]{1,0:T(8,128)(2,1)S(1)} %add.28), channel_id=1, source_target_pairs={{0,64},{32,96},{64,128},{96,160},{128,192},{160,224},{192,256},{22... | collective-permute-start | bytes 786440 | tf_op jit(solution)/shard_map/ppermute | solution.py:27
  236.4 0.1 add.33
  236.5 2.5 %collective-permute-start.29 = (bf16[128,1024]{1,0:T(8,128)(2,1)S(1)}, bf16[128,1024]{1,0:T(8,128)(2,1)S(1)}, u32[]{:S(2)}, u32[]{:S(2)}) collective-permute-start(bf16[128,1024]{1,0:T(8,128)(2,1)S(1)} %add.33), channel_id=1, source_target_pairs={{0,32},{32,0},{64,96},{96,64},{128,160},{160,128},{192,224},{224,1... | collective-permute-start | bytes 786440 | tf_op jit(solution)/shard_map/ppermute | solution.py:32
  239.0 0.0 collective-permute-done.21.second
  239.0 3.3 %collective-permute-done.18.first = bf16[128,1024]{1,0:T(8,128)(2,1)S(1)} collective-permute-done((bf16[128,1024]{1,0:T(8,128)(2,1)S(1)}, bf16[128,1024]{1,0:T(8,128)(2,1)S(1)}, u32[]{:S(2)}, u32[]{:S(2)}) %collective-permute-start.18) | collective-permute-done | bytes 262176 | tf_op jit(solution)/shard_map/ppermute | solution.py:27
  242.3 0.1 mine.1
  242.4 2.3 collective-permute-done.29.away
  244.7 0.9 last.1
  245.6 1.5 finish.1
  (91 shorter events, 0.2 us)
Async XLA Ops:
  4.6 159.2 %all-to-all-start = ((bf16[32,8,6144]{2,1,0:T(8,128)(2,1)}), bf16[32,8,6144]{2,1,0:T(8,128)(2,1)S(1)}, u32[]{:S(2)}, u32[]{:S(2)}) async-start(bf16[32,8,6144]{2,1,0:T(8,128)(2,1)} %bitcast.17), calls=%async_computation | async-start | bytes 6291456 | tf_op jit(solution)/shard_map/all_to_all | solution.py:342
  14.8 77.6 %collective-permute-start = (bf16[128,1536]{1,0:T(8,128)(2,1)}, bf16[128,1536]{1,0:T(8,128)(2,1)S(1)}, u32[]{:S(2)}, u32[]{:S(2)}) collective-permute-start(bf16[128,1536]{1,0:T(8,128)(2,1)} %get-tuple-element.28.refs_0_), channel_id=1, source_target_pairs={{0,32},{32,0},{64,96},{96,64},{128,160},{160,128},{192,224},{224,1... | collective-permute-start | bytes 1179656 | tf_op jit(solution)/shard_map/ppermute | solution.py:32
  17.4 88.4 %collective-permute-start.1 = (bf16[128,1536]{1,0:T(8,128)(2,1)}, bf16[128,1536]{1,0:T(8,128)(2,1)S(1)}, u32[]{:S(2)}, u32[]{:S(2)}) collective-permute-start(bf16[128,1536]{1,0:T(8,128)(2,1)} %get-tuple-element.28.refs_0_), channel_id=1, source_target_pairs={{0,64},{32,96},{64,128},{96,160},{128,192},{160,224},{192,256},{22... | collective-permute-start | bytes 1179656 | tf_op jit(solution)/shard_map/ppermute | solution.py:27
  92.5 16.8 %copy-start.30 = (bf16[128,1536]{1,0:T(8,128)(2,1)}, bf16[128,1536]{1,0:T(8,128)(2,1)S(1)}, u32[]{:S(2)}) copy-start(bf16[128,1536]{1,0:T(8,128)(2,1)S(1)} %collective-permute-done.refs_1_) | copy-start | bytes 1179652
  92.5 20.4 %collective-permute-start.4 = (bf16[128,1536]{1,0:T(8,128)(2,1)S(1)}, bf16[128,1536]{1,0:T(8,128)(2,1)S(1)}, u32[]{:S(2)}, u32[]{:S(2)}) collective-permute-start(bf16[128,1536]{1,0:T(8,128)(2,1)S(1)} %collective-permute-done.refs_1_), channel_id=1, source_target_pairs={{0,448},{32,480},{64,0},{96,32},{128,64},{160,96},{192,128},{224,1... | collective-permute-start | bytes 1179656 | tf_op jit(solution)/shard_map/ppermute | solution.py:27
  103.4 18.0 %collective-permute-start.2 = (bf16[128,1536]{1,0:T(8,128)(2,1)}, bf16[128,1536]{1,0:T(8,128)(2,1)S(1)}, u32[]{:S(2)}, u32[]{:S(2)}) collective-permute-start(bf16[128,1536]{1,0:T(8,128)(2,1)} %get-tuple-element.28.refs_0_), channel_id=1, source_target_pairs={{0,448},{32,480},{64,0},{96,32},{128,64},{160,96},{192,128},{224,1... | collective-permute-start | bytes 1179656 | tf_op jit(solution)/shard_map/ppermute | solution.py:27
  105.9 23.0 %copy-start.31 = (bf16[128,1536]{1,0:T(8,128)(2,1)}, bf16[128,1536]{1,0:T(8,128)(2,1)S(1)}, u32[]{:S(2)}) copy-start(bf16[128,1536]{1,0:T(8,128)(2,1)S(1)} %collective-permute-done.1.refs_2_) | copy-start | bytes 1179652
  105.9 21.0 %collective-permute-start.5 = (bf16[128,1536]{1,0:T(8,128)(2,1)S(1)}, bf16[128,1536]{1,0:T(8,128)(2,1)S(1)}, u32[]{:S(2)}, u32[]{:S(2)}) collective-permute-start(bf16[128,1536]{1,0:T(8,128)(2,1)S(1)} %collective-permute-done.1.refs_2_), channel_id=1, source_target_pairs={{0,64},{32,96},{64,128},{96,160},{128,192},{160,224},{192,256},{22... | collective-permute-start | bytes 1179656 | tf_op jit(solution)/shard_map/ppermute | solution.py:27
  109.3 19.6 %collective-permute-start.3 = (bf16[128,1536]{1,0:T(8,128)(2,1)S(1)}, bf16[128,1536]{1,0:T(8,128)(2,1)S(1)}, u32[]{:S(2)}, u32[]{:S(2)}) collective-permute-start(bf16[128,1536]{1,0:T(8,128)(2,1)S(1)} %collective-permute-done.refs_1_), channel_id=1, source_target_pairs={{0,64},{32,96},{64,128},{96,160},{128,192},{160,224},{192,256},{22... | collective-permute-start | bytes 1179656 | tf_op jit(solution)/shard_map/ppermute | solution.py:27
  112.9 17.9 %copy-start.32 = (bf16[128,1536]{1,0:T(8,128)(2,1)}, bf16[128,1536]{1,0:T(8,128)(2,1)S(1)}, u32[]{:S(2)}) copy-start(bf16[128,1536]{1,0:T(8,128)(2,1)S(1)} %collective-permute-done.4.refs_5_) | copy-start | bytes 1179652
  112.9 17.9 %collective-permute-start.8 = (bf16[128,1536]{1,0:T(8,128)(2,1)S(1)}, bf16[128,1536]{1,0:T(8,128)(2,1)S(1)}, u32[]{:S(2)}, u32[]{:S(2)}) collective-permute-start(bf16[128,1536]{1,0:T(8,128)(2,1)S(1)} %collective-permute-done.4.refs_5_), channel_id=1, source_target_pairs={{0,448},{32,480},{64,0},{96,32},{128,64},{160,96},{192,128},{224,1... | collective-permute-start | bytes 1179656 | tf_op jit(solution)/shard_map/ppermute | solution.py:27
  121.4 9.4 %copy-start.33 = (bf16[128,1536]{1,0:T(8,128)(2,1)}, bf16[128,1536]{1,0:T(8,128)(2,1)S(1)}, u32[]{:S(2)}) copy-start(bf16[128,1536]{1,0:T(8,128)(2,1)S(1)} %collective-permute-done.2.refs_3_) | copy-start | bytes 1179652
  121.4 16.7 %collective-permute-start.6 = (bf16[128,1536]{1,0:T(8,128)(2,1)S(1)}, bf16[128,1536]{1,0:T(8,128)(2,1)}, u32[]{:S(2)}, u32[]{:S(2)}) collective-permute-start(bf16[128,1536]{1,0:T(8,128)(2,1)S(1)} %collective-permute-done.2.refs_3_), channel_id=1, source_target_pairs={{0,448},{32,480},{64,0},{96,32},{128,64},{160,96},{192,128},{224,1... | collective-permute-start | bytes 1179656 | tf_op jit(solution)/shard_map/ppermute | solution.py:27
  126.9 11.2 %copy-start.34 = (bf16[128,1536]{1,0:T(8,128)(2,1)}, bf16[128,1536]{1,0:T(8,128)(2,1)S(1)}, u32[]{:S(2)}) copy-start(bf16[128,1536]{1,0:T(8,128)(2,1)S(1)} %collective-permute-done.5.refs_6_) | copy-start | bytes 1179652
  126.9 16.9 %collective-permute-start.9 = (bf16[128,1536]{1,0:T(8,128)(2,1)S(1)}, bf16[128,1536]{1,0:T(8,128)(2,1)}, u32[]{:S(2)}, u32[]{:S(2)}) collective-permute-start(bf16[128,1536]{1,0:T(8,128)(2,1)S(1)} %collective-permute-done.5.refs_6_), channel_id=1, source_target_pairs={{0,64},{32,96},{64,128},{96,160},{128,192},{160,224},{192,256},{22... | collective-permute-start | bytes 1179656 | tf_op jit(solution)/shard_map/ppermute | solution.py:27
  128.9 15.0 %copy-start.35 = (bf16[128,1536]{1,0:T(8,128)(2,1)}, bf16[128,1536]{1,0:T(8,128)(2,1)S(1)}, u32[]{:S(2)}) copy-start(bf16[128,1536]{1,0:T(8,128)(2,1)S(1)} %collective-permute-done.3.refs_4_) | copy-start | bytes 1179652
  128.9 17.7 %collective-permute-start.7 = (bf16[128,1536]{1,0:T(8,128)(2,1)S(1)}, bf16[128,1536]{1,0:T(8,128)(2,1)}, u32[]{:S(2)}, u32[]{:S(2)}) collective-permute-start(bf16[128,1536]{1,0:T(8,128)(2,1)S(1)} %collective-permute-done.3.refs_4_), channel_id=1, source_target_pairs={{0,64},{32,96},{64,128},{96,160},{128,192},{160,224},{192,256},{22... | collective-permute-start | bytes 1179656 | tf_op jit(solution)/shard_map/ppermute | solution.py:27
  130.9 15.7 %copy-start.36 = (bf16[128,1536]{1,0:T(8,128)(2,1)}, bf16[128,1536]{1,0:T(8,128)(2,1)S(1)}, u32[]{:S(2)}) copy-start(bf16[128,1536]{1,0:T(8,128)(2,1)S(1)} %collective-permute-done.8.refs_9_) | copy-start | bytes 1179652
  130.9 17.6 %collective-permute-start.12 = (bf16[128,1536]{1,0:T(8,128)(2,1)S(1)}, bf16[128,1536]{1,0:T(8,128)(2,1)}, u32[]{:S(2)}, u32[]{:S(2)}) collective-permute-start(bf16[128,1536]{1,0:T(8,128)(2,1)S(1)} %collective-permute-done.8.refs_9_), channel_id=1, source_target_pairs={{0,448},{32,480},{64,0},{96,32},{128,64},{160,96},{192,128},{224,1... | collective-permute-start | bytes 1179656 | tf_op jit(solution)/shard_map/ppermute | solution.py:27
  138.2 17.0 %collective-permute-start.10 = (bf16[128,1536]{1,0:T(8,128)(2,1)}, bf16[128,1536]{1,0:T(8,128)(2,1)}, u32[]{:S(2)}, u32[]{:S(2)}) collective-permute-start(bf16[128,1536]{1,0:T(8,128)(2,1)} %collective-permute-done.6.refs_7_), channel_id=1, source_target_pairs={{0,448},{32,480},{64,0},{96,32},{128,64},{160,96},{192,128},{224,1... | collective-permute-start | bytes 1179656 | tf_op jit(solution)/shard_map/ppermute | solution.py:27
  143.9 15.4 %collective-permute-start.13 = (bf16[128,1536]{1,0:T(8,128)(2,1)}, bf16[128,1536]{1,0:T(8,128)(2,1)}, u32[]{:S(2)}, u32[]{:S(2)}) collective-permute-start(bf16[128,1536]{1,0:T(8,128)(2,1)} %collective-permute-done.9.refs_10_), channel_id=1, source_target_pairs={{0,64},{32,96},{64,128},{96,160},{128,192},{160,224},{192,256},{22... | collective-permute-start | bytes 1179656 | tf_op jit(solution)/shard_map/ppermute | solution.py:27
  146.6 17.2 %collective-permute-start.11 = (bf16[128,1536]{1,0:T(8,128)(2,1)}, bf16[128,1536]{1,0:T(8,128)(2,1)}, u32[]{:S(2)}, u32[]{:S(2)}) collective-permute-start(bf16[128,1536]{1,0:T(8,128)(2,1)} %collective-permute-done.7.refs_8_), channel_id=1, source_target_pairs={{0,64},{32,96},{64,128},{96,160},{128,192},{160,224},{192,256},{22... | collective-permute-start | bytes 1179656 | tf_op jit(solution)/shard_map/ppermute | solution.py:27
  148.5 15.2 %collective-permute-start.14 = (bf16[128,1536]{1,0:T(8,128)(2,1)}, bf16[128,1536]{1,0:T(8,128)(2,1)}, u32[]{:S(2)}, u32[]{:S(2)}) collective-permute-start(bf16[128,1536]{1,0:T(8,128)(2,1)} %collective-permute-done.12.refs_13_), channel_id=1, source_target_pairs={{0,448},{32,480},{64,0},{96,32},{128,64},{160,96},{192,128},{224,1... | collective-permute-start | bytes 1179656 | tf_op jit(solution)/shard_map/ppermute | solution.py:27
  172.7 3.7 %copy-start.1 = (bf16[128,1024]{1,0:T(8,128)(2,1)}, bf16[128,1024]{1,0:T(8,128)(2,1)S(1)}, u32[]{:S(2)}) copy-start(bf16[128,1024]{1,0:T(8,128)(2,1)S(1)} %get-tuple-element.32.refs_0_) | copy-start | bytes 786436
  172.7 3.7 %copy-start.3 = (bf16[128,1024]{1,0:T(8,128)(2,1)}, bf16[128,1024]{1,0:T(8,128)(2,1)S(1)}, u32[]{:S(2)}) copy-start(bf16[128,1024]{1,0:T(8,128)(2,1)S(1)} %get-tuple-element.36.refs_0_) | copy-start | bytes 786436
  172.7 3.7 %copy-start.5 = (bf16[128,1024]{1,0:T(8,128)(2,1)}, bf16[128,1024]{1,0:T(8,128)(2,1)S(1)}, u32[]{:S(2)}) copy-start(bf16[128,1024]{1,0:T(8,128)(2,1)S(1)} %get-tuple-element.43.refs_0_) | copy-start | bytes 786436
  172.8 3.7 %copy-start.7 = (bf16[128,1024]{1,0:T(8,128)(2,1)}, bf16[128,1024]{1,0:T(8,128)(2,1)S(1)}, u32[]{:S(2)}) copy-start(bf16[128,1024]{1,0:T(8,128)(2,1)S(1)} %get-tuple-element.40.refs_0_) | copy-start | bytes 786436
  172.8 3.7 %copy-start.9 = (bf16[128,1024]{1,0:T(8,128)(2,1)}, bf16[128,1024]{1,0:T(8,128)(2,1)S(1)}, u32[]{:S(2)}) copy-start(bf16[128,1024]{1,0:T(8,128)(2,1)S(1)} %get-tuple-element.33.refs_0_) | copy-start | bytes 786436
  172.8 3.7 %copy-start.11 = (bf16[128,1024]{1,0:T(8,128)(2,1)}, bf16[128,1024]{1,0:T(8,128)(2,1)S(1)}, u32[]{:S(2)}) copy-start(bf16[128,1024]{1,0:T(8,128)(2,1)S(1)} %get-tuple-element.37) | copy-start | bytes 786436
  172.8 3.7 %copy-start.13 = (bf16[128,1024]{1,0:T(8,128)(2,1)}, bf16[128,1024]{1,0:T(8,128)(2,1)S(1)}, u32[]{:S(2)}) copy-start(bf16[128,1024]{1,0:T(8,128)(2,1)S(1)} %get-tuple-element.44.refs_0_) | copy-start | bytes 786436
  172.8 3.7 %copy-start.15 = (bf16[128,1024]{1,0:T(8,128)(2,1)}, bf16[128,1024]{1,0:T(8,128)(2,1)S(1)}, u32[]{:S(2)}) copy-start(bf16[128,1024]{1,0:T(8,128)(2,1)S(1)} %get-tuple-element.41) | copy-start | bytes 786436
  172.8 3.7 %copy-start.17 = (bf16[128,1024]{1,0:T(8,128)(2,1)}, bf16[128,1024]{1,0:T(8,128)(2,1)S(1)}, u32[]{:S(2)}) copy-start(bf16[128,1024]{1,0:T(8,128)(2,1)S(1)} %get-tuple-element.34) | copy-start | bytes 786436
  172.8 3.7 %copy-start.19 = (bf16[128,1024]{1,0:T(8,128)(2,1)}, bf16[128,1024]{1,0:T(8,128)(2,1)S(1)}, u32[]{:S(2)}) copy-start(bf16[128,1024]{1,0:T(8,128)(2,1)S(1)} %get-tuple-element.45) | copy-start | bytes 786436
  172.8 3.7 %copy-start.21 = (bf16[128,1024]{1,0:T(8,128)(2,1)}, bf16[128,1024]{1,0:T(8,128)(2,1)S(1)}, u32[]{:S(2)}) copy-start(bf16[128,1024]{1,0:T(8,128)(2,1)S(1)} %get-tuple-element.39.refs_0_) | copy-start | bytes 786436
  176.6 16.3 %copy-start.26 = (bf16[128,1024]{1,0:T(8,128)(2,1)S(1)}, bf16[128,1024]{1,0:T(8,128)(2,1)}, u32[]{:S(2)}) copy-start(bf16[128,1024]{1,0:T(8,128)(2,1)} %copy-done.25) | copy-start | bytes 786436
  176.6 23.2 %copy-start.20 = (bf16[128,1024]{1,0:T(8,128)(2,1)S(1)}, bf16[128,1024]{1,0:T(8,128)(2,1)}, u32[]{:S(2)}) copy-start(bf16[128,1024]{1,0:T(8,128)(2,1)} %copy-done.19) | copy-start | bytes 786436
  176.6 28.4 %copy-start.18 = (bf16[128,1024]{1,0:T(8,128)(2,1)S(1)}, bf16[128,1024]{1,0:T(8,128)(2,1)}, u32[]{:S(2)}) copy-start(bf16[128,1024]{1,0:T(8,128)(2,1)} %copy-done.17) | copy-start | bytes 786436
  176.6 32.0 %copy-start.16 = (bf16[128,1024]{1,0:T(8,128)(2,1)S(1)}, bf16[128,1024]{1,0:T(8,128)(2,1)}, u32[]{:S(2)}) copy-start(bf16[128,1024]{1,0:T(8,128)(2,1)} %copy-done.15) | copy-start | bytes 786436
  176.6 40.2 %copy-start.12 = (bf16[128,1024]{1,0:T(8,128)(2,1)S(1)}, bf16[128,1024]{1,0:T(8,128)(2,1)}, u32[]{:S(2)}) copy-start(bf16[128,1024]{1,0:T(8,128)(2,1)} %copy-done.11) | copy-start | bytes 786436
  176.6 42.7 %copy-start.10 = (bf16[128,1024]{1,0:T(8,128)(2,1)S(1)}, bf16[128,1024]{1,0:T(8,128)(2,1)}, u32[]{:S(2)}) copy-start(bf16[128,1024]{1,0:T(8,128)(2,1)} %copy-done.9) | copy-start | bytes 786436
  176.6 69.0 %all-to-all-start.1 = ((bf16[32,8,3072]{2,1,0:T(8,128)(2,1)}), bf16[32,8,3072]{2,1,0:T(8,128)(2,1)S(1)}, u32[]{:S(2)}, u32[]{:S(2)}) async-start(bf16[32,8,3072]{2,1,0:T(8,128)(2,1)} %bitcast.9), calls=%async_computation.1 | async-start | bytes 3145728 | tf_op jit(solution)/shard_map/all_to_all | solution.py:371
  186.8 36.1 %copy-start.8 = (bf16[128,1024]{1,0:T(8,128)(2,1)S(1)}, bf16[128,1024]{1,0:T(8,128)(2,1)}, u32[]{:S(2)}) copy-start(bf16[128,1024]{1,0:T(8,128)(2,1)} %copy-done.7) | copy-start | bytes 786436
  186.8 38.2 %copy-start.6 = (bf16[128,1024]{1,0:T(8,128)(2,1)S(1)}, bf16[128,1024]{1,0:T(8,128)(2,1)}, u32[]{:S(2)}) copy-start(bf16[128,1024]{1,0:T(8,128)(2,1)} %copy-done.5) | copy-start | bytes 786436
  186.8 12.9 %collective-permute-start.25 = (bf16[128,1024]{1,0:T(8,128)(2,1)}, bf16[128,1024]{1,0:T(8,128)(2,1)S(1)}, u32[]{:S(2)}, u32[]{:S(2)}) collective-permute-start(bf16[128,1024]{1,0:T(8,128)(2,1)} %copy-done.29), channel_id=1, source_target_pairs={{0,448},{32,480},{64,0},{96,32},{128,64},{160,96},{192,128},{224,1... | collective-permute-start | bytes 786440 | tf_op jit(solution)/shard_map/ppermute | solution.py:27
  190.7 14.3 %collective-permute-start.15 = (bf16[128,1024]{1,0:T(8,128)(2,1)}, bf16[128,1024]{1,0:T(8,128)(2,1)S(1)}, u32[]{:S(2)}, u32[]{:S(2)}) collective-permute-start(bf16[128,1024]{1,0:T(8,128)(2,1)} %copy-done.28), channel_id=1, source_target_pairs={{0,64},{32,96},{64,128},{96,160},{128,192},{160,224},{192,256},{22... | collective-permute-start | bytes 786440 | tf_op jit(solution)/shard_map/ppermute | solution.py:27
  192.8 24.0 %collective-permute-start.19 = (bf16[128,1024]{1,0:T(8,128)(2,1)S(1)}, bf16[128,1024]{1,0:T(8,128)(2,1)S(1)}, u32[]{:S(2)}, u32[]{:S(2)}) collective-permute-start(bf16[128,1024]{1,0:T(8,128)(2,1)S(1)} %copy-done.26), channel_id=1, source_target_pairs={{0,448},{32,480},{64,0},{96,32},{128,64},{160,96},{192,128},{224,1... | collective-permute-start | bytes 786440 | tf_op jit(solution)/shard_map/ppermute | solution.py:27
  197.8 10.8 %collective-permute-start.22 = (bf16[128,1024]{1,0:T(8,128)(2,1)}, bf16[128,1024]{1,0:T(8,128)(2,1)S(1)}, u32[]{:S(2)}, u32[]{:S(2)}) collective-permute-start(bf16[128,1024]{1,0:T(8,128)(2,1)} %copy-done.27), channel_id=1, source_target_pairs={{0,64},{32,96},{64,128},{96,160},{128,192},{160,224},{192,256},{22... | collective-permute-start | bytes 786440 | tf_op jit(solution)/shard_map/ppermute | solution.py:27
  199.8 30.5 %copy-start.4 = (bf16[128,1024]{1,0:T(8,128)(2,1)S(1)}, bf16[128,1024]{1,0:T(8,128)(2,1)}, u32[]{:S(2)}) copy-start(bf16[128,1024]{1,0:T(8,128)(2,1)} %copy-done.3) | copy-start | bytes 786436
  199.9 10.8 %collective-permute-start.26 = (bf16[128,1024]{1,0:T(8,128)(2,1)S(1)}, bf16[128,1024]{1,0:T(8,128)(2,1)S(1)}, u32[]{:S(2)}, u32[]{:S(2)}) collective-permute-start(bf16[128,1024]{1,0:T(8,128)(2,1)S(1)} %add_convert_fusion), channel_id=1, source_target_pairs={{0,448},{32,480},{64,0},{96,32},{128,64},{160,96},{192,128},{224,1... | collective-permute-start | bytes 786440 | tf_op jit(solution)/shard_map/ppermute | solution.py:27
  205.0 27.7 %copy-start.2 = (bf16[128,1024]{1,0:T(8,128)(2,1)S(1)}, bf16[128,1024]{1,0:T(8,128)(2,1)}, u32[]{:S(2)}) copy-start(bf16[128,1024]{1,0:T(8,128)(2,1)} %copy-done.1) | copy-start | bytes 786436
  205.1 14.2 %collective-permute-start.16 = (bf16[128,1024]{1,0:T(8,128)(2,1)S(1)}, bf16[128,1024]{1,0:T(8,128)(2,1)S(1)}, u32[]{:S(2)}, u32[]{:S(2)}) collective-permute-start(bf16[128,1024]{1,0:T(8,128)(2,1)S(1)} %add_convert_fusion.3), channel_id=1, source_target_pairs={{0,64},{32,96},{64,128},{96,160},{128,192},{160,224},{192,256},{22... | collective-permute-start | bytes 786440 | tf_op jit(solution)/shard_map/ppermute | solution.py:27
  208.6 27.7 %copy-start.22 = (bf16[128,1024]{1,0:T(8,128)(2,1)S(1)}, bf16[128,1024]{1,0:T(8,128)(2,1)}, u32[]{:S(2)}) copy-start(bf16[128,1024]{1,0:T(8,128)(2,1)} %copy-done.21) | copy-start | bytes 786436
  208.7 14.2 %collective-permute-start.23 = (bf16[128,1024]{1,0:T(8,128)(2,1)S(1)}, bf16[128,1024]{1,0:T(8,128)(2,1)S(1)}, u32[]{:S(2)}, u32[]{:S(2)}) collective-permute-start(bf16[128,1024]{1,0:T(8,128)(2,1)S(1)} %add_convert_fusion.1), channel_id=1, source_target_pairs={{0,64},{32,96},{64,128},{96,160},{128,192},{160,224},{192,256},{22... | collective-permute-start | bytes 786440 | tf_op jit(solution)/shard_map/ppermute | solution.py:27
  211.7 13.4 %collective-permute-start.27 = (bf16[128,1024]{1,0:T(8,128)(2,1)S(1)}, bf16[128,1024]{1,0:T(8,128)(2,1)S(1)}, u32[]{:S(2)}, u32[]{:S(2)}) collective-permute-start(bf16[128,1024]{1,0:T(8,128)(2,1)S(1)} %add.31), channel_id=1, source_target_pairs={{0,448},{32,480},{64,0},{96,32},{128,64},{160,96},{192,128},{224,1... | collective-permute-start | bytes 786440 | tf_op jit(solution)/shard_map/ppermute | solution.py:27
  216.9 13.4 %collective-permute-start.20 = (bf16[128,1024]{1,0:T(8,128)(2,1)S(1)}, bf16[128,1024]{1,0:T(8,128)(2,1)S(1)}, u32[]{:S(2)}, u32[]{:S(2)}) collective-permute-start(bf16[128,1024]{1,0:T(8,128)(2,1)S(1)} %add_convert_fusion.2), channel_id=1, source_target_pairs={{0,448},{32,480},{64,0},{96,32},{128,64},{160,96},{192,128},{224,1... | collective-permute-start | bytes 786440 | tf_op jit(solution)/shard_map/ppermute | solution.py:27
  219.4 13.4 %collective-permute-start.17 = (bf16[128,1024]{1,0:T(8,128)(2,1)S(1)}, bf16[128,1024]{1,0:T(8,128)(2,1)S(1)}, u32[]{:S(2)}, u32[]{:S(2)}) collective-permute-start(bf16[128,1024]{1,0:T(8,128)(2,1)S(1)} %add.27), channel_id=1, source_target_pairs={{0,64},{32,96},{64,128},{96,160},{128,192},{160,224},{192,256},{22... | collective-permute-start | bytes 786440 | tf_op jit(solution)/shard_map/ppermute | solution.py:27
  222.9 22.7 %copy-start = (bf16[128,2048]{1,0:T(8,128)(2,1)S(1)}, bf16[128,2048]{1,0:T(8,128)(2,1)}, u32[]{:S(2)}) copy-start(bf16[128,2048]{1,0:T(8,128)(2,1)} %tokens.1) | copy-start | bytes 1572868
  222.9 22.7 %copy-start.23 = (bf16[256,384]{1,0:T(8,128)(2,1)S(1)}, bf16[256,384]{1,0:T(8,128)(2,1)}, u32[]{:S(2)}) copy-start(bf16[256,384]{1,0:T(8,128)(2,1)} %get-tuple-element.26.select) | copy-start | bytes 589828
  222.9 22.7 %copy-start.24 = (f32[2048]{0:T(1024)S(1)}, f32[2048]{0:T(1024)}, u32[]{:S(2)}) copy-start(f32[2048]{0:T(1024)} %param.9) | copy-start | bytes 24580
  223.0 13.3 %collective-permute-start.24 = (bf16[128,1024]{1,0:T(8,128)(2,1)S(1)}, bf16[128,1024]{1,0:T(8,128)(2,1)S(1)}, u32[]{:S(2)}, u32[]{:S(2)}) collective-permute-start(bf16[128,1024]{1,0:T(8,128)(2,1)S(1)} %add.30), channel_id=1, source_target_pairs={{0,64},{32,96},{64,128},{96,160},{128,192},{160,224},{192,256},{22... | collective-permute-start | bytes 786440 | tf_op jit(solution)/shard_map/ppermute | solution.py:27
  225.1 11.2 %collective-permute-start.28 = (bf16[128,1024]{1,0:T(8,128)(2,1)S(1)}, bf16[128,1024]{1,0:T(8,128)(2,1)S(1)}, u32[]{:S(2)}, u32[]{:S(2)}) collective-permute-start(bf16[128,1024]{1,0:T(8,128)(2,1)S(1)} %add.32), channel_id=1, source_target_pairs={{0,448},{32,480},{64,0},{96,32},{128,64},{160,96},{192,128},{224,1... | collective-permute-start | bytes 786440 | tf_op jit(solution)/shard_map/ppermute | solution.py:27
  230.4 8.7 %collective-permute-start.21 = (bf16[128,1024]{1,0:T(8,128)(2,1)S(1)}, bf16[128,1024]{1,0:T(8,128)(2,1)S(1)}, u32[]{:S(2)}, u32[]{:S(2)}) collective-permute-start(bf16[128,1024]{1,0:T(8,128)(2,1)S(1)} %add.29), channel_id=1, source_target_pairs={{0,448},{32,480},{64,0},{96,32},{128,64},{160,96},{192,128},{224,1... | collective-permute-start | bytes 786440 | tf_op jit(solution)/shard_map/ppermute | solution.py:27
  232.8 9.5 %collective-permute-start.18 = (bf16[128,1024]{1,0:T(8,128)(2,1)S(1)}, bf16[128,1024]{1,0:T(8,128)(2,1)S(1)}, u32[]{:S(2)}, u32[]{:S(2)}) collective-permute-start(bf16[128,1024]{1,0:T(8,128)(2,1)S(1)} %add.28), channel_id=1, source_target_pairs={{0,64},{32,96},{64,128},{96,160},{128,192},{160,224},{192,256},{22... | collective-permute-start | bytes 786440 | tf_op jit(solution)/shard_map/ppermute | solution.py:27
  236.5 8.3 %collective-permute-start.29 = (bf16[128,1024]{1,0:T(8,128)(2,1)S(1)}, bf16[128,1024]{1,0:T(8,128)(2,1)S(1)}, u32[]{:S(2)}, u32[]{:S(2)}) collective-permute-start(bf16[128,1024]{1,0:T(8,128)(2,1)S(1)} %add.33), channel_id=1, source_target_pairs={{0,32},{32,0},{64,96},{96,64},{128,160},{160,128},{192,224},{224,1... | collective-permute-start | bytes 786440 | tf_op jit(solution)/shard_map/ppermute | solution.py:32
  (5 other events, 15.7 us)

commit v2 on v1

--- a/solution.py
+++ b/solution.py
@@ -196,17 +196,32 @@
         piece[...] = parts[spot(index, step, other, block_rows), :]
 
 
-def back_kernel(grad_pre, weights, back):
+def back_kernel(grad_pre, weights, back_far, back, sems):
     rows = grad_pre.shape[0]
     width, both = weights.shape
     half = width // 2
     col_col = ((1,), (1,))
-    back[:, 0:width] = dot(grad_pre[:, 0:both], weights[:, 0:both], col_col).astype(BF)
+    stores = []
+
+    def ship(start):
+        here = slice(start, start + half)
+        stores.append(
+            pltpu.make_async_copy(back.at[:, here], back_far.at[:, here], sems.at[len(stores)])
+        )
+        stores[-1].start()
+
     high = grad_pre[:, both : 2 * both]
     left = dot(high, weights[0:half, 0:both], col_col)
     right = dot(high, weights[half:width, 0:both], col_col)
     pick = lax.broadcasted_iota(jnp.int32, (rows, half), 0) % LOW < HALF
     back[:, width : width + half] = jnp.where(pick, left, right).astype(BF)
+    ship(width)
+    for start in (0, half):
+        part = dot(grad_pre[:, 0:both], weights[start : start + half, 0:both], col_col)
+        back[:, start : start + half] = part.astype(BF)
+        ship(start)
+    for copy in stores:
+        copy.wait()
 
 
 def finish_kernel(tokens, gain, select, back, out):
@@ -365,6 +380,11 @@
     back = pl.pallas_call(
         back_kernel,
         out_shape=jax.ShapeDtypeStruct((experts * LOW, width + width // 2), BF),
+        out_specs=there,
+        scratch_shapes=[
+            pltpu.VMEM((experts * LOW, width + width // 2), BF),
+            pltpu.SemaphoreType.DMA((3,)),
+        ],
         compiler_params=limit(16),
         name="back",
     )(*near(grad_pre, both))

time: 248 us -> 248 us (level)
  no operation moved by 1% of the time
where the time goes in v2:
time: 248 us; the launch traced here: 247 us
  starting transfers between devices  129 us (52%)
  waiting for transfers between devices  95.6 us (39%)
  Pallas kernels  19.1 us (8%)
    ppermute x28, starting transfers between devices, shift_z(): return lax.ppermute(value, 'grp', pairs)  104 us
    ppermute x2, waiting for transfers between devices, swap_y(): return lax.ppermute(value, 'grp', pairs)  73.1 us
    ppermute x28, waiting for transfers between devices, shift_z(): return lax.ppermute(value, 'grp', pairs)  22.5 us
    all_to_all x1, starting transfers between devices, body(): lax.all_to_all(send.reshape(experts, LOW, 3 * width), 'ep', split_axis=0,...  10.2 us
    all_to_all x1, starting transfers between devices, body(): lax.all_to_all(back.reshape(experts, LOW, width + width // 2), 'ep', spli...  10.2 us
    pallas_call x1, Pallas kernels, body(): pl.pallas_call(functools.partial(expert_kernel, places), out_shape=[pltpu...  8.95 us
    ppermute x2, starting transfers between devices, swap_y(): return lax.ppermute(value, 'grp', pairs)  5.13 us
  transfers between devices with their start and end apart: 32, of which 11 were waited for; matrix products, arithmetic and copies ran while one was open for 0% of the time, Pallas kernels for 1%

profile of v2, /device:TPU:6, one launch (start us, length us, event | category | flops | bytes accessed | tf_op | source)
XLA Modules:
  0.0 246.9 jit_solution(2935949851688346936)
XLA Ops:
  0.6 3.9 %dispatch.1 = (bf16[256,6144]{1,0:T(8,128)(2,1)}, bf16[256,384]{1,0:T(8,128)(2,1)}, bf16[128,1536]{1,0:T(8,128)(2,1)}) custom-call(bf16[128,2048]{1,0:T(8,128)(2,1)} %tokens.1, f32[1,2048]{1,0:T(1,128)} %bitcast.15, s32[2,128]{1,0:T(2,128)} %bitcast.21, f32[2,128]{1,0:T(2,128)} %bitcast.22, bf16[128,2048]{1,0:T(8,128)(2,1)} %refs_4_.1, ...), custom_call_target="tpu_custom_call" | custom-call | tf_op jit(solution)/shard_map/dispatch/pallas_call | solution.py:333
  4.6 10.2 %all-to-all-start = ((bf16[32,8,6144]{2,1,0:T(8,128)(2,1)}), bf16[32,8,6144]{2,1,0:T(8,128)(2,1)S(1)}, u32[]{:S(2)}, u32[]{:S(2)}) async-start(bf16[32,8,6144]{2,1,0:T(8,128)(2,1)} %bitcast.17), calls=%async_computation | async-start | bytes 6291456 | tf_op jit(solution)/shard_map/all_to_all | solution.py:357
  14.8 2.6 %collective-permute-start = (bf16[128,1536]{1,0:T(8,128)(2,1)}, bf16[128,1536]{1,0:T(8,128)(2,1)S(1)}, u32[]{:S(2)}, u32[]{:S(2)}) collective-permute-start(bf16[128,1536]{1,0:T(8,128)(2,1)} %get-tuple-element.28.refs_0_), channel_id=1, source_target_pairs={{0,32},{32,0},{64,96},{96,64},{128,160},{160,128},{192,224},{224,1... | collective-permute-start | bytes 1179656 | tf_op jit(solution)/shard_map/ppermute | solution.py:32
  17.4 4.3 %collective-permute-start.1 = (bf16[128,1536]{1,0:T(8,128)(2,1)}, bf16[128,1536]{1,0:T(8,128)(2,1)S(1)}, u32[]{:S(2)}, u32[]{:S(2)}) collective-permute-start(bf16[128,1536]{1,0:T(8,128)(2,1)} %get-tuple-element.28.refs_0_), channel_id=1, source_target_pairs={{0,64},{32,96},{64,128},{96,160},{128,192},{160,224},{192,256},{22... | collective-permute-start | bytes 1179656 | tf_op jit(solution)/shard_map/ppermute | solution.py:27
  21.7 70.8 %collective-permute-done.refs_1_ = bf16[128,1536]{1,0:T(8,128)(2,1)S(1)} collective-permute-done((bf16[128,1536]{1,0:T(8,128)(2,1)}, bf16[128,1536]{1,0:T(8,128)(2,1)S(1)}, u32[]{:S(2)}, u32[]{:S(2)}) %collective-permute-start) | collective-permute-done | bytes 393248 | tf_op jit(solution)/shard_map/ppermute | solution.py:32
  92.5 10.9 %collective-permute-start.4 = (bf16[128,1536]{1,0:T(8,128)(2,1)S(1)}, bf16[128,1536]{1,0:T(8,128)(2,1)S(1)}, u32[]{:S(2)}, u32[]{:S(2)}) collective-permute-start(bf16[128,1536]{1,0:T(8,128)(2,1)S(1)} %collective-permute-done.refs_1_), channel_id=1, source_target_pairs={{0,448},{32,480},{64,0},{96,32},{128,64},{160,96},{192,128},{224,1... | collective-permute-start | bytes 1179656 | tf_op jit(solution)/shard_map/ppermute | solution.py:27
  103.4 2.5 collective-permute-start.2
  105.9 3.4 %collective-permute-start.5 = (bf16[128,1536]{1,0:T(8,128)(2,1)S(1)}, bf16[128,1536]{1,0:T(8,128)(2,1)S(1)}, u32[]{:S(2)}, u32[]{:S(2)}) collective-permute-start(bf16[128,1536]{1,0:T(8,128)(2,1)S(1)} %collective-permute-done.1.refs_2_), channel_id=1, source_target_pairs={{0,64},{32,96},{64,128},{96,160},{128,192},{160,224},{192,256},{22... | collective-permute-start | bytes 1179656 | tf_op jit(solution)/shard_map/ppermute | solution.py:27
  109.3 1.9 collective-permute-start.3
  111.2 1.7 collective-permute-done.4.refs_5_
  112.9 5.6 %collective-permute-start.8 = (bf16[128,1536]{1,0:T(8,128)(2,1)S(1)}, bf16[128,1536]{1,0:T(8,128)(2,1)S(1)}, u32[]{:S(2)}, u32[]{:S(2)}) collective-permute-start(bf16[128,1536]{1,0:T(8,128)(2,1)S(1)} %collective-permute-done.4.refs_5_), channel_id=1, source_target_pairs={{0,448},{32,480},{64,0},{96,32},{128,64},{160,96},{192,128},{224,1... | collective-permute-start | bytes 1179656 | tf_op jit(solution)/shard_map/ppermute | solution.py:27
  118.5 2.9 %collective-permute-done.2.refs_3_ = bf16[128,1536]{1,0:T(8,128)(2,1)S(1)} collective-permute-done((bf16[128,1536]{1,0:T(8,128)(2,1)}, bf16[128,1536]{1,0:T(8,128)(2,1)S(1)}, u32[]{:S(2)}, u32[]{:S(2)}) %collective-permute-start.2) | collective-permute-done | bytes 393248 | tf_op jit(solution)/shard_map/ppermute | solution.py:27
  121.4 5.5 %collective-permute-start.6 = (bf16[128,1536]{1,0:T(8,128)(2,1)S(1)}, bf16[128,1536]{1,0:T(8,128)(2,1)}, u32[]{:S(2)}, u32[]{:S(2)}) collective-permute-start(bf16[128,1536]{1,0:T(8,128)(2,1)S(1)} %collective-permute-done.2.refs_3_), channel_id=1, source_target_pairs={{0,448},{32,480},{64,0},{96,32},{128,64},{160,96},{192,128},{224,1... | collective-permute-start | bytes 1179656 | tf_op jit(solution)/shard_map/ppermute | solution.py:27
  126.9 1.9 collective-permute-start.9
  128.9 1.9 collective-permute-start.7
  130.9 5.1 %collective-permute-start.12 = (bf16[128,1536]{1,0:T(8,128)(2,1)S(1)}, bf16[128,1536]{1,0:T(8,128)(2,1)}, u32[]{:S(2)}, u32[]{:S(2)}) collective-permute-start(bf16[128,1536]{1,0:T(8,128)(2,1)S(1)} %collective-permute-done.8.refs_9_), channel_id=1, source_target_pairs={{0,448},{32,480},{64,0},{96,32},{128,64},{160,96},{192,128},{224,1... | collective-permute-start | bytes 1179656 | tf_op jit(solution)/shard_map/ppermute | solution.py:27
  136.0 2.2 collective-permute-done.6.refs_7_
  138.2 5.7 %collective-permute-start.10 = (bf16[128,1536]{1,0:T(8,128)(2,1)}, bf16[128,1536]{1,0:T(8,128)(2,1)}, u32[]{:S(2)}, u32[]{:S(2)}) collective-permute-start(bf16[128,1536]{1,0:T(8,128)(2,1)} %collective-permute-done.6.refs_7_), channel_id=1, source_target_pairs={{0,448},{32,480},{64,0},{96,32},{128,64},{160,96},{192,128},{224,1... | collective-permute-start | bytes 1179656 | tf_op jit(solution)/shard_map/ppermute | solution.py:27
  143.9 1.9 collective-permute-start.13
  145.8 0.8 collective-permute-done.7.refs_8_
  146.6 1.9 collective-permute-start.11
  148.5 5.1 %collective-permute-start.14 = (bf16[128,1536]{1,0:T(8,128)(2,1)}, bf16[128,1536]{1,0:T(8,128)(2,1)}, u32[]{:S(2)}, u32[]{:S(2)}) collective-permute-start(bf16[128,1536]{1,0:T(8,128)(2,1)} %collective-permute-done.12.refs_13_), channel_id=1, source_target_pairs={{0,448},{32,480},{64,0},{96,32},{128,64},{160,96},{192,128},{224,1... | collective-permute-start | bytes 1179656 | tf_op jit(solution)/shard_map/ppermute | solution.py:27
  153.7 1.5 collective-permute-done.10.refs_11_
  155.1 4.2 %collective-permute-done.13.refs_14_ = bf16[128,1536]{1,0:T(8,128)(2,1)} collective-permute-done((bf16[128,1536]{1,0:T(8,128)(2,1)}, bf16[128,1536]{1,0:T(8,128)(2,1)}, u32[]{:S(2)}, u32[]{:S(2)}) %collective-permute-start.13) | collective-permute-done | bytes 393248 | tf_op jit(solution)/shard_map/ppermute | solution.py:27
  159.3 4.4 %collective-permute-done.11.refs_12_ = bf16[128,1536]{1,0:T(8,128)(2,1)} collective-permute-done((bf16[128,1536]{1,0:T(8,128)(2,1)}, bf16[128,1536]{1,0:T(8,128)(2,1)}, u32[]{:S(2)}, u32[]{:S(2)}) %collective-permute-start.11) | collective-permute-done | bytes 393248 | tf_op jit(solution)/shard_map/ppermute | solution.py:27
  163.8 9.0 %expert.1 = (bf16[256,2048]{1,0:T(8,128)(2,1)S(1)}, bf16[2048,1024]{1,0:T(8,128)(2,1)S(1)}, bf16[128,1024]{1,0:T(8,128)(2,1)S(1)}, bf16[128,1024]{1,0:T(8,128)(2...) custom-call(s32[1]{0:T(128)} %bitcast.6.where, ...), custom_call_target="tpu_custom_call" | custom-call | tf_op jit(solution)/shard_map/expert/pallas_call | solution.py:362
  172.7 0.0 copy-start.1
  172.9 3.2 %back.1 = bf16[256,3072]{1,0:T(8,128)(2,1)} custom-call(bf16[256,2048]{1,0:T(8,128)(2,1)S(1)} %get-tuple-element.29.grad_pre, bf16[2048,1024]{1,0:T(8,128)(2,1)S(1)} %get-tuple-element.30.weights), custom_call_target="tpu_custom_call" | custom-call | tf_op jit(solution)/shard_map/back/pallas_call | solution.py:380
  176.3 10.2 %all-to-all-start.1 = ((bf16[32,8,3072]{2,1,0:T(8,128)(2,1)}), bf16[32,8,3072]{2,1,0:T(8,128)(2,1)S(1)}, u32[]{:S(2)}, u32[]{:S(2)}) async-start(bf16[32,8,3072]{2,1,0:T(8,128)(2,1)} %bitcast.9), calls=%async_computation.1 | async-start | bytes 3145728 | tf_op jit(solution)/shard_map/all_to_all | solution.py:391
  186.5 3.9 %collective-permute-start.25 = (bf16[128,1024]{1,0:T(8,128)(2,1)}, bf16[128,1024]{1,0:T(8,128)(2,1)S(1)}, u32[]{:S(2)}, u32[]{:S(2)}) collective-permute-start(bf16[128,1024]{1,0:T(8,128)(2,1)} %copy-done.29), channel_id=1, source_target_pairs={{0,448},{32,480},{64,0},{96,32},{128,64},{160,96},{192,128},{224,1... | collective-permute-start | bytes 786440 | tf_op jit(solution)/shard_map/ppermute | solution.py:27
  190.5 2.1 collective-permute-start.15
  192.5 5.0 %collective-permute-start.19 = (bf16[128,1024]{1,0:T(8,128)(2,1)S(1)}, bf16[128,1024]{1,0:T(8,128)(2,1)S(1)}, u32[]{:S(2)}, u32[]{:S(2)}) collective-permute-start(bf16[128,1024]{1,0:T(8,128)(2,1)S(1)} %copy-done.26), channel_id=1, source_target_pairs={{0,448},{32,480},{64,0},{96,32},{128,64},{160,96},{192,128},{224,1... | collective-permute-start | bytes 786440 | tf_op jit(solution)/shard_map/ppermute | solution.py:27
  197.5 1.9 collective-permute-start.22
  199.5 0.1 add_convert_fusion
  199.6 5.1 %collective-permute-start.26 = (bf16[128,1024]{1,0:T(8,128)(2,1)S(1)}, bf16[128,1024]{1,0:T(8,128)(2,1)S(1)}, u32[]{:S(2)}, u32[]{:S(2)}) collective-permute-start(bf16[128,1024]{1,0:T(8,128)(2,1)S(1)} %add_convert_fusion), channel_id=1, source_target_pairs={{0,448},{32,480},{64,0},{96,32},{128,64},{160,96},{192,128},{224,1... | collective-permute-start | bytes 786440 | tf_op jit(solution)/shard_map/ppermute | solution.py:27
  204.7 0.0 copy-start.2
  204.7 0.1 add_convert_fusion.3
  204.8 1.9 collective-permute-start.16
  206.7 1.6 collective-permute-done.22
  208.3 0.1 add_convert_fusion.1
  208.4 1.9 collective-permute-start.23
  210.4 0.9 copy-done.14
  211.3 0.1 add.31
  211.4 5.1 %collective-permute-start.27 = (bf16[128,1024]{1,0:T(8,128)(2,1)S(1)}, bf16[128,1024]{1,0:T(8,128)(2,1)S(1)}, u32[]{:S(2)}, u32[]{:S(2)}) collective-permute-start(bf16[128,1024]{1,0:T(8,128)(2,1)S(1)} %add.31), channel_id=1, source_target_pairs={{0,448},{32,480},{64,0},{96,32},{128,64},{160,96},{192,128},{224,1... | collective-permute-start | bytes 786440 | tf_op jit(solution)/shard_map/ppermute | solution.py:27
  216.5 0.1 add_convert_fusion.2
  216.6 2.4 collective-permute-start.20
  219.0 0.1 add.27
  219.1 3.5 %collective-permute-start.17 = (bf16[128,1024]{1,0:T(8,128)(2,1)S(1)}, bf16[128,1024]{1,0:T(8,128)(2,1)S(1)}, u32[]{:S(2)}, u32[]{:S(2)}) collective-permute-start(bf16[128,1024]{1,0:T(8,128)(2,1)S(1)} %add.27), channel_id=1, source_target_pairs={{0,64},{32,96},{64,128},{96,160},{128,192},{160,224},{192,256},{22... | collective-permute-start | bytes 786440 | tf_op jit(solution)/shard_map/ppermute | solution.py:27
  222.6 0.1 add.30
  222.7 2.1 collective-permute-start.24
  224.8 0.1 add.32
  224.8 5.1 %collective-permute-start.28 = (bf16[128,1024]{1,0:T(8,128)(2,1)S(1)}, bf16[128,1024]{1,0:T(8,128)(2,1)S(1)}, u32[]{:S(2)}, u32[]{:S(2)}) collective-permute-start(bf16[128,1024]{1,0:T(8,128)(2,1)S(1)} %add.32), channel_id=1, source_target_pairs={{0,448},{32,480},{64,0},{96,32},{128,64},{160,96},{192,128},{224,1... | collective-permute-start | bytes 786440 | tf_op jit(solution)/shard_map/ppermute | solution.py:27
  230.0 0.1 add.29
  230.1 2.4 collective-permute-start.21
  232.5 0.1 add.28
  232.5 3.5 %collective-permute-start.18 = (bf16[128,1024]{1,0:T(8,128)(2,1)S(1)}, bf16[128,1024]{1,0:T(8,128)(2,1)S(1)}, u32[]{:S(2)}, u32[]{:S(2)}) collective-permute-start(bf16[128,1024]{1,0:T(8,128)(2,1)S(1)} %add.28), channel_id=1, source_target_pairs={{0,64},{32,96},{64,128},{96,160},{128,192},{160,224},{192,256},{22... | collective-permute-start | bytes 786440 | tf_op jit(solution)/shard_map/ppermute | solution.py:27
  236.1 0.1 add.33
  236.2 2.5 %collective-permute-start.29 = (bf16[128,1024]{1,0:T(8,128)(2,1)S(1)}, bf16[128,1024]{1,0:T(8,128)(2,1)S(1)}, u32[]{:S(2)}, u32[]{:S(2)}) collective-permute-start(bf16[128,1024]{1,0:T(8,128)(2,1)S(1)} %add.33), channel_id=1, source_target_pairs={{0,32},{32,0},{64,96},{96,64},{128,160},{160,128},{192,224},{224,1... | collective-permute-start | bytes 786440 | tf_op jit(solution)/shard_map/ppermute | solution.py:32
  238.7 0.0 collective-permute-done.21.second
  238.7 3.3 %collective-permute-done.18.first = bf16[128,1024]{1,0:T(8,128)(2,1)S(1)} collective-permute-done((bf16[128,1024]{1,0:T(8,128)(2,1)S(1)}, bf16[128,1024]{1,0:T(8,128)(2,1)S(1)}, u32[]{:S(2)}, u32[]{:S(2)}) %collective-permute-start.18) | collective-permute-done | bytes 262176 | tf_op jit(solution)/shard_map/ppermute | solution.py:27
  242.0 0.1 mine.1
  242.1 2.3 collective-permute-done.29.away
  244.4 0.9 last.1
  245.4 1.5 finish.1
  (91 shorter events, 0.2 us)
Async XLA Ops:
  4.6 159.2 %all-to-all-start = ((bf16[32,8,6144]{2,1,0:T(8,128)(2,1)}), bf16[32,8,6144]{2,1,0:T(8,128)(2,1)S(1)}, u32[]{:S(2)}, u32[]{:S(2)}) async-start(bf16[32,8,6144]{2,1,0:T(8,128)(2,1)} %bitcast.17), calls=%async_computation | async-start | bytes 6291456 | tf_op jit(solution)/shard_map/all_to_all | solution.py:357
  14.8 77.6 %collective-permute-start = (bf16[128,1536]{1,0:T(8,128)(2,1)}, bf16[128,1536]{1,0:T(8,128)(2,1)S(1)}, u32[]{:S(2)}, u32[]{:S(2)}) collective-permute-start(bf16[128,1536]{1,0:T(8,128)(2,1)} %get-tuple-element.28.refs_0_), channel_id=1, source_target_pairs={{0,32},{32,0},{64,96},{96,64},{128,160},{160,128},{192,224},{224,1... | collective-permute-start | bytes 1179656 | tf_op jit(solution)/shard_map/ppermute | solution.py:32
  17.4 88.4 %collective-permute-start.1 = (bf16[128,1536]{1,0:T(8,128)(2,1)}, bf16[128,1536]{1,0:T(8,128)(2,1)S(1)}, u32[]{:S(2)}, u32[]{:S(2)}) collective-permute-start(bf16[128,1536]{1,0:T(8,128)(2,1)} %get-tuple-element.28.refs_0_), channel_id=1, source_target_pairs={{0,64},{32,96},{64,128},{96,160},{128,192},{160,224},{192,256},{22... | collective-permute-start | bytes 1179656 | tf_op jit(solution)/shard_map/ppermute | solution.py:27
  92.5 16.8 %copy-start.30 = (bf16[128,1536]{1,0:T(8,128)(2,1)}, bf16[128,1536]{1,0:T(8,128)(2,1)S(1)}, u32[]{:S(2)}) copy-start(bf16[128,1536]{1,0:T(8,128)(2,1)S(1)} %collective-permute-done.refs_1_) | copy-start | bytes 1179652
  92.5 20.4 %collective-permute-start.4 = (bf16[128,1536]{1,0:T(8,128)(2,1)S(1)}, bf16[128,1536]{1,0:T(8,128)(2,1)S(1)}, u32[]{:S(2)}, u32[]{:S(2)}) collective-permute-start(bf16[128,1536]{1,0:T(8,128)(2,1)S(1)} %collective-permute-done.refs_1_), channel_id=1, source_target_pairs={{0,448},{32,480},{64,0},{96,32},{128,64},{160,96},{192,128},{224,1... | collective-permute-start | bytes 1179656 | tf_op jit(solution)/shard_map/ppermute | solution.py:27
  103.4 18.0 %collective-permute-start.2 = (bf16[128,1536]{1,0:T(8,128)(2,1)}, bf16[128,1536]{1,0:T(8,128)(2,1)S(1)}, u32[]{:S(2)}, u32[]{:S(2)}) collective-permute-start(bf16[128,1536]{1,0:T(8,128)(2,1)} %get-tuple-element.28.refs_0_), channel_id=1, source_target_pairs={{0,448},{32,480},{64,0},{96,32},{128,64},{160,96},{192,128},{224,1... | collective-permute-start | bytes 1179656 | tf_op jit(solution)/shard_map/ppermute | solution.py:27
  105.9 23.0 %copy-start.31 = (bf16[128,1536]{1,0:T(8,128)(2,1)}, bf16[128,1536]{1,0:T(8,128)(2,1)S(1)}, u32[]{:S(2)}) copy-start(bf16[128,1536]{1,0:T(8,128)(2,1)S(1)} %collective-permute-done.1.refs_2_) | copy-start | bytes 1179652
  105.9 21.0 %collective-permute-start.5 = (bf16[128,1536]{1,0:T(8,128)(2,1)S(1)}, bf16[128,1536]{1,0:T(8,128)(2,1)S(1)}, u32[]{:S(2)}, u32[]{:S(2)}) collective-permute-start(bf16[128,1536]{1,0:T(8,128)(2,1)S(1)} %collective-permute-done.1.refs_2_), channel_id=1, source_target_pairs={{0,64},{32,96},{64,128},{96,160},{128,192},{160,224},{192,256},{22... | collective-permute-start | bytes 1179656 | tf_op jit(solution)/shard_map/ppermute | solution.py:27
  109.3 19.6 %collective-permute-start.3 = (bf16[128,1536]{1,0:T(8,128)(2,1)S(1)}, bf16[128,1536]{1,0:T(8,128)(2,1)S(1)}, u32[]{:S(2)}, u32[]{:S(2)}) collective-permute-start(bf16[128,1536]{1,0:T(8,128)(2,1)S(1)} %collective-permute-done.refs_1_), channel_id=1, source_target_pairs={{0,64},{32,96},{64,128},{96,160},{128,192},{160,224},{192,256},{22... | collective-permute-start | bytes 1179656 | tf_op jit(solution)/shard_map/ppermute | solution.py:27
  112.9 17.9 %copy-start.32 = (bf16[128,1536]{1,0:T(8,128)(2,1)}, bf16[128,1536]{1,0:T(8,128)(2,1)S(1)}, u32[]{:S(2)}) copy-start(bf16[128,1536]{1,0:T(8,128)(2,1)S(1)} %collective-permute-done.4.refs_5_) | copy-start | bytes 1179652
  112.9 17.9 %collective-permute-start.8 = (bf16[128,1536]{1,0:T(8,128)(2,1)S(1)}, bf16[128,1536]{1,0:T(8,128)(2,1)S(1)}, u32[]{:S(2)}, u32[]{:S(2)}) collective-permute-start(bf16[128,1536]{1,0:T(8,128)(2,1)S(1)} %collective-permute-done.4.refs_5_), channel_id=1, source_target_pairs={{0,448},{32,480},{64,0},{96,32},{128,64},{160,96},{192,128},{224,1... | collective-permute-start | bytes 1179656 | tf_op jit(solution)/shard_map/ppermute | solution.py:27
  121.4 9.4 %copy-start.33 = (bf16[128,1536]{1,0:T(8,128)(2,1)}, bf16[128,1536]{1,0:T(8,128)(2,1)S(1)}, u32[]{:S(2)}) copy-start(bf16[128,1536]{1,0:T(8,128)(2,1)S(1)} %collective-permute-done.2.refs_3_) | copy-start | bytes 1179652
  121.4 16.7 %collective-permute-start.6 = (bf16[128,1536]{1,0:T(8,128)(2,1)S(1)}, bf16[128,1536]{1,0:T(8,128)(2,1)}, u32[]{:S(2)}, u32[]{:S(2)}) collective-permute-start(bf16[128,1536]{1,0:T(8,128)(2,1)S(1)} %collective-permute-done.2.refs_3_), channel_id=1, source_target_pairs={{0,448},{32,480},{64,0},{96,32},{128,64},{160,96},{192,128},{224,1... | collective-permute-start | bytes 1179656 | tf_op jit(solution)/shard_map/ppermute | solution.py:27
  126.9 11.2 %copy-start.34 = (bf16[128,1536]{1,0:T(8,128)(2,1)}, bf16[128,1536]{1,0:T(8,128)(2,1)S(1)}, u32[]{:S(2)}) copy-start(bf16[128,1536]{1,0:T(8,128)(2,1)S(1)} %collective-permute-done.5.refs_6_) | copy-start | bytes 1179652
  126.9 16.9 %collective-permute-start.9 = (bf16[128,1536]{1,0:T(8,128)(2,1)S(1)}, bf16[128,1536]{1,0:T(8,128)(2,1)}, u32[]{:S(2)}, u32[]{:S(2)}) collective-permute-start(bf16[128,1536]{1,0:T(8,128)(2,1)S(1)} %collective-permute-done.5.refs_6_), channel_id=1, source_target_pairs={{0,64},{32,96},{64,128},{96,160},{128,192},{160,224},{192,256},{22... | collective-permute-start | bytes 1179656 | tf_op jit(solution)/shard_map/ppermute | solution.py:27
  128.9 15.0 %copy-start.35 = (bf16[128,1536]{1,0:T(8,128)(2,1)}, bf16[128,1536]{1,0:T(8,128)(2,1)S(1)}, u32[]{:S(2)}) copy-start(bf16[128,1536]{1,0:T(8,128)(2,1)S(1)} %collective-permute-done.3.refs_4_) | copy-start | bytes 1179652
  128.9 17.7 %collective-permute-start.7 = (bf16[128,1536]{1,0:T(8,128)(2,1)S(1)}, bf16[128,1536]{1,0:T(8,128)(2,1)}, u32[]{:S(2)}, u32[]{:S(2)}) collective-permute-start(bf16[128,1536]{1,0:T(8,128)(2,1)S(1)} %collective-permute-done.3.refs_4_), channel_id=1, source_target_pairs={{0,64},{32,96},{64,128},{96,160},{128,192},{160,224},{192,256},{22... | collective-permute-start | bytes 1179656 | tf_op jit(solution)/shard_map/ppermute | solution.py:27
  130.9 15.7 %copy-start.36 = (bf16[128,1536]{1,0:T(8,128)(2,1)}, bf16[128,1536]{1,0:T(8,128)(2,1)S(1)}, u32[]{:S(2)}) copy-start(bf16[128,1536]{1,0:T(8,128)(2,1)S(1)} %collective-permute-done.8.refs_9_) | copy-start | bytes 1179652
  130.9 17.6 %collective-permute-start.12 = (bf16[128,1536]{1,0:T(8,128)(2,1)S(1)}, bf16[128,1536]{1,0:T(8,128)(2,1)}, u32[]{:S(2)}, u32[]{:S(2)}) collective-permute-start(bf16[128,1536]{1,0:T(8,128)(2,1)S(1)} %collective-permute-done.8.refs_9_), channel_id=1, source_target_pairs={{0,448},{32,480},{64,0},{96,32},{128,64},{160,96},{192,128},{224,1... | collective-permute-start | bytes 1179656 | tf_op jit(solution)/shard_map/ppermute | solution.py:27
  138.2 17.0 %collective-permute-start.10 = (bf16[128,1536]{1,0:T(8,128)(2,1)}, bf16[128,1536]{1,0:T(8,128)(2,1)}, u32[]{:S(2)}, u32[]{:S(2)}) collective-permute-start(bf16[128,1536]{1,0:T(8,128)(2,1)} %collective-permute-done.6.refs_7_), channel_id=1, source_target_pairs={{0,448},{32,480},{64,0},{96,32},{128,64},{160,96},{192,128},{224,1... | collective-permute-start | bytes 1179656 | tf_op jit(solution)/shard_map/ppermute | solution.py:27
  143.9 15.4 %collective-permute-start.13 = (bf16[128,1536]{1,0:T(8,128)(2,1)}, bf16[128,1536]{1,0:T(8,128)(2,1)}, u32[]{:S(2)}, u32[]{:S(2)}) collective-permute-start(bf16[128,1536]{1,0:T(8,128)(2,1)} %collective-permute-done.9.refs_10_), channel_id=1, source_target_pairs={{0,64},{32,96},{64,128},{96,160},{128,192},{160,224},{192,256},{22... | collective-permute-start | bytes 1179656 | tf_op jit(solution)/shard_map/ppermute | solution.py:27
  146.6 17.2 %collective-permute-start.11 = (bf16[128,1536]{1,0:T(8,128)(2,1)}, bf16[128,1536]{1,0:T(8,128)(2,1)}, u32[]{:S(2)}, u32[]{:S(2)}) collective-permute-start(bf16[128,1536]{1,0:T(8,128)(2,1)} %collective-permute-done.7.refs_8_), channel_id=1, source_target_pairs={{0,64},{32,96},{64,128},{96,160},{128,192},{160,224},{192,256},{22... | collective-permute-start | bytes 1179656 | tf_op jit(solution)/shard_map/ppermute | solution.py:27
  148.5 15.2 %collective-permute-start.14 = (bf16[128,1536]{1,0:T(8,128)(2,1)}, bf16[128,1536]{1,0:T(8,128)(2,1)}, u32[]{:S(2)}, u32[]{:S(2)}) collective-permute-start(bf16[128,1536]{1,0:T(8,128)(2,1)} %collective-permute-done.12.refs_13_), channel_id=1, source_target_pairs={{0,448},{32,480},{64,0},{96,32},{128,64},{160,96},{192,128},{224,1... | collective-permute-start | bytes 1179656 | tf_op jit(solution)/shard_map/ppermute | solution.py:27
  172.7 3.4 %copy-start.1 = (bf16[128,1024]{1,0:T(8,128)(2,1)}, bf16[128,1024]{1,0:T(8,128)(2,1)S(1)}, u32[]{:S(2)}) copy-start(bf16[128,1024]{1,0:T(8,128)(2,1)S(1)} %get-tuple-element.32.refs_0_) | copy-start | bytes 786436
  172.7 3.4 %copy-start.3 = (bf16[128,1024]{1,0:T(8,128)(2,1)}, bf16[128,1024]{1,0:T(8,128)(2,1)S(1)}, u32[]{:S(2)}) copy-start(bf16[128,1024]{1,0:T(8,128)(2,1)S(1)} %get-tuple-element.36.refs_0_) | copy-start | bytes 786436
  172.7 3.4 %copy-start.5 = (bf16[128,1024]{1,0:T(8,128)(2,1)}, bf16[128,1024]{1,0:T(8,128)(2,1)S(1)}, u32[]{:S(2)}) copy-start(bf16[128,1024]{1,0:T(8,128)(2,1)S(1)} %get-tuple-element.43.refs_0_) | copy-start | bytes 786436
  172.8 3.4 %copy-start.7 = (bf16[128,1024]{1,0:T(8,128)(2,1)}, bf16[128,1024]{1,0:T(8,128)(2,1)S(1)}, u32[]{:S(2)}) copy-start(bf16[128,1024]{1,0:T(8,128)(2,1)S(1)} %get-tuple-element.40.refs_0_) | copy-start | bytes 786436
  172.8 3.4 %copy-start.9 = (bf16[128,1024]{1,0:T(8,128)(2,1)}, bf16[128,1024]{1,0:T(8,128)(2,1)S(1)}, u32[]{:S(2)}) copy-start(bf16[128,1024]{1,0:T(8,128)(2,1)S(1)} %get-tuple-element.33.refs_0_) | copy-start | bytes 786436
  172.8 3.4 %copy-start.11 = (bf16[128,1024]{1,0:T(8,128)(2,1)}, bf16[128,1024]{1,0:T(8,128)(2,1)S(1)}, u32[]{:S(2)}) copy-start(bf16[128,1024]{1,0:T(8,128)(2,1)S(1)} %get-tuple-element.37) | copy-start | bytes 786436
  172.8 3.4 %copy-start.13 = (bf16[128,1024]{1,0:T(8,128)(2,1)}, bf16[128,1024]{1,0:T(8,128)(2,1)S(1)}, u32[]{:S(2)}) copy-start(bf16[128,1024]{1,0:T(8,128)(2,1)S(1)} %get-tuple-element.44.refs_0_) | copy-start | bytes 786436
  172.8 3.4 %copy-start.15 = (bf16[128,1024]{1,0:T(8,128)(2,1)}, bf16[128,1024]{1,0:T(8,128)(2,1)S(1)}, u32[]{:S(2)}) copy-start(bf16[128,1024]{1,0:T(8,128)(2,1)S(1)} %get-tuple-element.41) | copy-start | bytes 786436
  172.8 3.4 %copy-start.17 = (bf16[128,1024]{1,0:T(8,128)(2,1)}, bf16[128,1024]{1,0:T(8,128)(2,1)S(1)}, u32[]{:S(2)}) copy-start(bf16[128,1024]{1,0:T(8,128)(2,1)S(1)} %get-tuple-element.34) | copy-start | bytes 786436
  172.8 3.4 %copy-start.19 = (bf16[128,1024]{1,0:T(8,128)(2,1)}, bf16[128,1024]{1,0:T(8,128)(2,1)S(1)}, u32[]{:S(2)}) copy-start(bf16[128,1024]{1,0:T(8,128)(2,1)S(1)} %get-tuple-element.45) | copy-start | bytes 786436
  172.8 3.4 %copy-start.21 = (bf16[128,1024]{1,0:T(8,128)(2,1)}, bf16[128,1024]{1,0:T(8,128)(2,1)S(1)}, u32[]{:S(2)}) copy-start(bf16[128,1024]{1,0:T(8,128)(2,1)S(1)} %get-tuple-element.39.refs_0_) | copy-start | bytes 786436
  176.3 16.3 %copy-start.26 = (bf16[128,1024]{1,0:T(8,128)(2,1)S(1)}, bf16[128,1024]{1,0:T(8,128)(2,1)}, u32[]{:S(2)}) copy-start(bf16[128,1024]{1,0:T(8,128)(2,1)} %copy-done.25) | copy-start | bytes 786436
  176.3 23.2 %copy-start.20 = (bf16[128,1024]{1,0:T(8,128)(2,1)S(1)}, bf16[128,1024]{1,0:T(8,128)(2,1)}, u32[]{:S(2)}) copy-start(bf16[128,1024]{1,0:T(8,128)(2,1)} %copy-done.19) | copy-start | bytes 786436
  176.3 28.4 %copy-start.18 = (bf16[128,1024]{1,0:T(8,128)(2,1)S(1)}, bf16[128,1024]{1,0:T(8,128)(2,1)}, u32[]{:S(2)}) copy-start(bf16[128,1024]{1,0:T(8,128)(2,1)} %copy-done.17) | copy-start | bytes 786436
  176.3 32.0 %copy-start.16 = (bf16[128,1024]{1,0:T(8,128)(2,1)S(1)}, bf16[128,1024]{1,0:T(8,128)(2,1)}, u32[]{:S(2)}) copy-start(bf16[128,1024]{1,0:T(8,128)(2,1)} %copy-done.15) | copy-start | bytes 786436
  176.3 40.2 %copy-start.12 = (bf16[128,1024]{1,0:T(8,128)(2,1)S(1)}, bf16[128,1024]{1,0:T(8,128)(2,1)}, u32[]{:S(2)}) copy-start(bf16[128,1024]{1,0:T(8,128)(2,1)} %copy-done.11) | copy-start | bytes 786436
  176.3 42.7 %copy-start.10 = (bf16[128,1024]{1,0:T(8,128)(2,1)S(1)}, bf16[128,1024]{1,0:T(8,128)(2,1)}, u32[]{:S(2)}) copy-start(bf16[128,1024]{1,0:T(8,128)(2,1)} %copy-done.9) | copy-start | bytes 786436
  176.3 69.0 %all-to-all-start.1 = ((bf16[32,8,3072]{2,1,0:T(8,128)(2,1)}), bf16[32,8,3072]{2,1,0:T(8,128)(2,1)S(1)}, u32[]{:S(2)}, u32[]{:S(2)}) async-start(bf16[32,8,3072]{2,1,0:T(8,128)(2,1)} %bitcast.9), calls=%async_computation.1 | async-start | bytes 3145728 | tf_op jit(solution)/shard_map/all_to_all | solution.py:391
  186.5 36.1 %copy-start.8 = (bf16[128,1024]{1,0:T(8,128)(2,1)S(1)}, bf16[128,1024]{1,0:T(8,128)(2,1)}, u32[]{:S(2)}) copy-start(bf16[128,1024]{1,0:T(8,128)(2,1)} %copy-done.7) | copy-start | bytes 786436
  186.5 38.2 %copy-start.6 = (bf16[128,1024]{1,0:T(8,128)(2,1)S(1)}, bf16[128,1024]{1,0:T(8,128)(2,1)}, u32[]{:S(2)}) copy-start(bf16[128,1024]{1,0:T(8,128)(2,1)} %copy-done.5) | copy-start | bytes 786436
  186.5 12.9 %collective-permute-start.25 = (bf16[128,1024]{1,0:T(8,128)(2,1)}, bf16[128,1024]{1,0:T(8,128)(2,1)S(1)}, u32[]{:S(2)}, u32[]{:S(2)}) collective-permute-start(bf16[128,1024]{1,0:T(8,128)(2,1)} %copy-done.29), channel_id=1, source_target_pairs={{0,448},{32,480},{64,0},{96,32},{128,64},{160,96},{192,128},{224,1... | collective-permute-start | bytes 786440 | tf_op jit(solution)/shard_map/ppermute | solution.py:27
  190.5 14.3 %collective-permute-start.15 = (bf16[128,1024]{1,0:T(8,128)(2,1)}, bf16[128,1024]{1,0:T(8,128)(2,1)S(1)}, u32[]{:S(2)}, u32[]{:S(2)}) collective-permute-start(bf16[128,1024]{1,0:T(8,128)(2,1)} %copy-done.28), channel_id=1, source_target_pairs={{0,64},{32,96},{64,128},{96,160},{128,192},{160,224},{192,256},{22... | collective-permute-start | bytes 786440 | tf_op jit(solution)/shard_map/ppermute | solution.py:27
  192.5 24.0 %collective-permute-start.19 = (bf16[128,1024]{1,0:T(8,128)(2,1)S(1)}, bf16[128,1024]{1,0:T(8,128)(2,1)S(1)}, u32[]{:S(2)}, u32[]{:S(2)}) collective-permute-start(bf16[128,1024]{1,0:T(8,128)(2,1)S(1)} %copy-done.26), channel_id=1, source_target_pairs={{0,448},{32,480},{64,0},{96,32},{128,64},{160,96},{192,128},{224,1... | collective-permute-start | bytes 786440 | tf_op jit(solution)/shard_map/ppermute | solution.py:27
  197.5 10.8 %collective-permute-start.22 = (bf16[128,1024]{1,0:T(8,128)(2,1)}, bf16[128,1024]{1,0:T(8,128)(2,1)S(1)}, u32[]{:S(2)}, u32[]{:S(2)}) collective-permute-start(bf16[128,1024]{1,0:T(8,128)(2,1)} %copy-done.27), channel_id=1, source_target_pairs={{0,64},{32,96},{64,128},{96,160},{128,192},{160,224},{192,256},{22... | collective-permute-start | bytes 786440 | tf_op jit(solution)/shard_map/ppermute | solution.py:27
  199.5 30.5 %copy-start.4 = (bf16[128,1024]{1,0:T(8,128)(2,1)S(1)}, bf16[128,1024]{1,0:T(8,128)(2,1)}, u32[]{:S(2)}) copy-start(bf16[128,1024]{1,0:T(8,128)(2,1)} %copy-done.3) | copy-start | bytes 786436
  199.6 10.8 %collective-permute-start.26 = (bf16[128,1024]{1,0:T(8,128)(2,1)S(1)}, bf16[128,1024]{1,0:T(8,128)(2,1)S(1)}, u32[]{:S(2)}, u32[]{:S(2)}) collective-permute-start(bf16[128,1024]{1,0:T(8,128)(2,1)S(1)} %add_convert_fusion), channel_id=1, source_target_pairs={{0,448},{32,480},{64,0},{96,32},{128,64},{160,96},{192,128},{224,1... | collective-permute-start | bytes 786440 | tf_op jit(solution)/shard_map/ppermute | solution.py:27
  204.7 27.7 %copy-start.2 = (bf16[128,1024]{1,0:T(8,128)(2,1)S(1)}, bf16[128,1024]{1,0:T(8,128)(2,1)}, u32[]{:S(2)}) copy-start(bf16[128,1024]{1,0:T(8,128)(2,1)} %copy-done.1) | copy-start | bytes 786436
  204.8 14.2 %collective-permute-start.16 = (bf16[128,1024]{1,0:T(8,128)(2,1)S(1)}, bf16[128,1024]{1,0:T(8,128)(2,1)S(1)}, u32[]{:S(2)}, u32[]{:S(2)}) collective-permute-start(bf16[128,1024]{1,0:T(8,128)(2,1)S(1)} %add_convert_fusion.3), channel_id=1, source_target_pairs={{0,64},{32,96},{64,128},{96,160},{128,192},{160,224},{192,256},{22... | collective-permute-start | bytes 786440 | tf_op jit(solution)/shard_map/ppermute | solution.py:27
  208.3 27.7 %copy-start.22 = (bf16[128,1024]{1,0:T(8,128)(2,1)S(1)}, bf16[128,1024]{1,0:T(8,128)(2,1)}, u32[]{:S(2)}) copy-start(bf16[128,1024]{1,0:T(8,128)(2,1)} %copy-done.21) | copy-start | bytes 786436
  208.4 14.2 %collective-permute-start.23 = (bf16[128,1024]{1,0:T(8,128)(2,1)S(1)}, bf16[128,1024]{1,0:T(8,128)(2,1)S(1)}, u32[]{:S(2)}, u32[]{:S(2)}) collective-permute-start(bf16[128,1024]{1,0:T(8,128)(2,1)S(1)} %add_convert_fusion.1), channel_id=1, source_target_pairs={{0,64},{32,96},{64,128},{96,160},{128,192},{160,224},{192,256},{22... | collective-permute-start | bytes 786440 | tf_op jit(solution)/shard_map/ppermute | solution.py:27
  211.4 13.4 %collective-permute-start.27 = (bf16[128,1024]{1,0:T(8,128)(2,1)S(1)}, bf16[128,1024]{1,0:T(8,128)(2,1)S(1)}, u32[]{:S(2)}, u32[]{:S(2)}) collective-permute-start(bf16[128,1024]{1,0:T(8,128)(2,1)S(1)} %add.31), channel_id=1, source_target_pairs={{0,448},{32,480},{64,0},{96,32},{128,64},{160,96},{192,128},{224,1... | collective-permute-start | bytes 786440 | tf_op jit(solution)/shard_map/ppermute | solution.py:27
  216.6 13.4 %collective-permute-start.20 = (bf16[128,1024]{1,0:T(8,128)(2,1)S(1)}, bf16[128,1024]{1,0:T(8,128)(2,1)S(1)}, u32[]{:S(2)}, u32[]{:S(2)}) collective-permute-start(bf16[128,1024]{1,0:T(8,128)(2,1)S(1)} %add_convert_fusion.2), channel_id=1, source_target_pairs={{0,448},{32,480},{64,0},{96,32},{128,64},{160,96},{192,128},{224,1... | collective-permute-start | bytes 786440 | tf_op jit(solution)/shard_map/ppermute | solution.py:27
  219.1 13.4 %collective-permute-start.17 = (bf16[128,1024]{1,0:T(8,128)(2,1)S(1)}, bf16[128,1024]{1,0:T(8,128)(2,1)S(1)}, u32[]{:S(2)}, u32[]{:S(2)}) collective-permute-start(bf16[128,1024]{1,0:T(8,128)(2,1)S(1)} %add.27), channel_id=1, source_target_pairs={{0,64},{32,96},{64,128},{96,160},{128,192},{160,224},{192,256},{22... | collective-permute-start | bytes 786440 | tf_op jit(solution)/shard_map/ppermute | solution.py:27
  222.6 22.7 %copy-start = (bf16[128,2048]{1,0:T(8,128)(2,1)S(1)}, bf16[128,2048]{1,0:T(8,128)(2,1)}, u32[]{:S(2)}) copy-start(bf16[128,2048]{1,0:T(8,128)(2,1)} %tokens.1) | copy-start | bytes 1572868
  222.6 22.7 %copy-start.23 = (bf16[256,384]{1,0:T(8,128)(2,1)S(1)}, bf16[256,384]{1,0:T(8,128)(2,1)}, u32[]{:S(2)}) copy-start(bf16[256,384]{1,0:T(8,128)(2,1)} %get-tuple-element.26.select) | copy-start | bytes 589828
  222.6 22.7 %copy-start.24 = (f32[2048]{0:T(1024)S(1)}, f32[2048]{0:T(1024)}, u32[]{:S(2)}) copy-start(f32[2048]{0:T(1024)} %param.9) | copy-start | bytes 24580
  222.7 13.3 %collective-permute-start.24 = (bf16[128,1024]{1,0:T(8,128)(2,1)S(1)}, bf16[128,1024]{1,0:T(8,128)(2,1)S(1)}, u32[]{:S(2)}, u32[]{:S(2)}) collective-permute-start(bf16[128,1024]{1,0:T(8,128)(2,1)S(1)} %add.30), channel_id=1, source_target_pairs={{0,64},{32,96},{64,128},{96,160},{128,192},{160,224},{192,256},{22... | collective-permute-start | bytes 786440 | tf_op jit(solution)/shard_map/ppermute | solution.py:27
  224.8 11.2 %collective-permute-start.28 = (bf16[128,1024]{1,0:T(8,128)(2,1)S(1)}, bf16[128,1024]{1,0:T(8,128)(2,1)S(1)}, u32[]{:S(2)}, u32[]{:S(2)}) collective-permute-start(bf16[128,1024]{1,0:T(8,128)(2,1)S(1)} %add.32), channel_id=1, source_target_pairs={{0,448},{32,480},{64,0},{96,32},{128,64},{160,96},{192,128},{224,1... | collective-permute-start | bytes 786440 | tf_op jit(solution)/shard_map/ppermute | solution.py:27
  230.1 8.7 %collective-permute-start.21 = (bf16[128,1024]{1,0:T(8,128)(2,1)S(1)}, bf16[128,1024]{1,0:T(8,128)(2,1)S(1)}, u32[]{:S(2)}, u32[]{:S(2)}) collective-permute-start(bf16[128,1024]{1,0:T(8,128)(2,1)S(1)} %add.29), channel_id=1, source_target_pairs={{0,448},{32,480},{64,0},{96,32},{128,64},{160,96},{192,128},{224,1... | collective-permute-start | bytes 786440 | tf_op jit(solution)/shard_map/ppermute | solution.py:27
  232.5 9.5 %collective-permute-start.18 = (bf16[128,1024]{1,0:T(8,128)(2,1)S(1)}, bf16[128,1024]{1,0:T(8,128)(2,1)S(1)}, u32[]{:S(2)}, u32[]{:S(2)}) collective-permute-start(bf16[128,1024]{1,0:T(8,128)(2,1)S(1)} %add.28), channel_id=1, source_target_pairs={{0,64},{32,96},{64,128},{96,160},{128,192},{160,224},{192,256},{22... | collective-permute-start | bytes 786440 | tf_op jit(solution)/shard_map/ppermute | solution.py:27
  236.2 8.3 %collective-permute-start.29 = (bf16[128,1024]{1,0:T(8,128)(2,1)S(1)}, bf16[128,1024]{1,0:T(8,128)(2,1)S(1)}, u32[]{:S(2)}, u32[]{:S(2)}) collective-permute-start(bf16[128,1024]{1,0:T(8,128)(2,1)S(1)} %add.33), channel_id=1, source_target_pairs={{0,32},{32,0},{64,96},{96,64},{128,160},{160,128},{192,224},{224,1... | collective-permute-start | bytes 786440 | tf_op jit(solution)/shard_map/ppermute | solution.py:32
  (5 other events, 14.5 us)
